TPU v7x, 32 devices: a whole 2x2x4 slice. The times are simulated.
32 devices in a mesh: gx: 4 (over z), gy: 2 (over y), gz: 4 (over x, core).
Axes of the slice: x: 2, y: 2, z: 4, core: 2. Of those that a mesh axis runs over, the one named last changes fastest.
Arguments:
- nodal_warmth_degrees: float32 [3, 3, 3, 16, 8, 512], P(None, None, None, 'gx', 'gy', 'gz'), may hold values from -6 to 6
- thermal_transfer_coefficient: float32 [16, 8, 512], P('gx', 'gy', 'gz'), may hold values from 0.1 to 2
- taken_beam_fraction: float32 [16, 8, 512], P('gx', 'gy', 'gz'), may hold values from 0.3 to 3
- laid_tiers: int32 [4, 2, 4], P('gx', 'gy', 'gz'), may hold values from 64 to 128
- holding_brick_column: int32 [4, 2, 4, 2048, 1], P('gx', 'gy', 'gz'), may hold values from 0 to 3; in each aligned block of 2048 rows (0 to 2047, 2048 to 4095, ..., all dimensions but the last counted through in order) at most 1024 rows name the same one
- piece_onto_solid_brick: int32 [4, 2, 4, 2048], P('gx', 'gy', 'gz'), may hold values from 0 to 255, as said below
- deformation_change: float32 [6, 8, 8192], P(None, None, ('gx', 'gy', 'gz')), may hold values from -0.06 to 0.06
- earlier_tension_state: float32 [6, 8, 8192], P(None, None, ('gx', 'gy', 'gz')), may hold values from -3 to 3
- plastic_onset_threshold: float32 [8192], P(('gx', 'gy', 'gz')), may hold values from 0.5 to 2
Outputs:
- temperature_new: float32 [3, 3, 3, 16, 8, 512], P(None, None, None, 'gx', 'gy', 'gz')
- stress_new: float32 [6, 8, 8192], P(None, None, ('gx', 'gy', 'gz'))
- forces: float32 [3, 8, 8192], P(None, None, ('gx', 'gy', 'gz'))
Inputs may be any that keep to these rules, and one draw needn't show every extreme that they name: `holding_brick_column`: the elements of one device hand at most 1024 elements to one owner; in every draw some device hands exactly 1024 to some owner. `piece_onto_solid_brick`: some mechanical cells may receive no element.
All inputs are finite; a program needn't handle non-finite values.
Results may differ from a plain program's by a relative error of at most 0.00022.
Values sent between devices are 32-bit elements; how exact they have to be, the bound alone decides.
A program may use at most 64 MiB of HBM per device.

v0:
```python
import math

import jax
import jax.numpy as jnp
import numpy as np
from jax import lax
from jax.sharding import PartitionSpec as P

STEPS = 4


time_step = 0.003
penalty = 3.0
heat_power = 100.0
expansion = 0.02
shear_modulus = 100.0 / 2.6
lame_first = 30.0 / 0.52
hardening = 10.0
highest = lax.Precision.HIGHEST
nodal_weights = np.array([1.0 / 6.0, 2.0 / 3.0, 1.0 / 6.0], np.float32)


def with_halo(cells, sides, width):
    for axis, dim in sides:
        count = lax.axis_size(axis)
        ends = count - 1
        head = lax.slice_in_dim(cells, 0, width, axis=dim)
        tail = lax.slice_in_dim(cells, cells.shape[dim] - width, cells.shape[dim], axis=dim)
        cells = jnp.concatenate(
            [
                lax.ppermute(tail, axis, [(i, (i + 1) % count) for i in range(ends)]),
                cells,
                lax.ppermute(head, axis, [((i + 1) % count, i) for i in range(ends)]),
            ],
            axis=dim,
        )
    return cells


def lumped_line():
    stiff = np.array([[7.0, -8.0, 1.0], [-8.0, 16.0, -8.0], [1.0, -8.0, 7.0]], np.float32) / 3.0
    return stiff / nodal_weights[:, None]


def gauss_spots():
    half = 0.5 / math.sqrt(3.0)
    return [0.5 - half, 0.5 + half]


def gauss_values():
    rows = []
    for point in gauss_spots():
        rows.append(
            [
                2.0 * (point - 0.5) * (point - 1.0),
                -4.0 * point * (point - 1.0),
                2.0 * point * (point - 0.5),
            ]
        )
    return np.array(rows, np.float32)


def gradient_table():
    spots = gauss_spots()
    table = np.zeros((3, 8, 8), np.float32)
    for node in range(8):
        corner = [node // 4, node // 2 % 2, node % 2]
        for point in range(8):
            place = [spots[point // 4], spots[point // 2 % 2], spots[point % 2]]
            values = [place[k] if corner[k] else 1.0 - place[k] for k in range(3)]
            slopes = [1.0 if corner[k] else -1.0 for k in range(3)]
            table[0, node, point] = slopes[0] * values[1] * values[2] / 8.0
            table[1, node, point] = values[0] * slopes[1] * values[2] / 8.0
            table[2, node, point] = values[0] * values[1] * slopes[2] / 8.0
    return table


def window(array, lead, axis, offset):
    index = [slice(None)] * lead
    for k in range(3):
        move = offset if k == axis else 0
        index.append(slice(1 + move, array.shape[lead + k] - 1 + move))
    return array[tuple(index)]


def node_terms(anchor, count, centre, near, far):
    places = (jnp.arange(count) + anchor).astype(jnp.float32)[None, :] + 0.5 * jnp.arange(3).astype(
        jnp.float32
    )[:, None]
    offset = places - centre
    radius = jnp.where(offset >= 0.0, near, far)
    return -3.0 * (offset / radius) ** 2


def volume_rate(core, kcore):
    line = jnp.asarray(lumped_line())
    rate = jnp.einsum("ai,ibcxyz->abcxyz", line, core, precision=highest)
    rate = rate + jnp.einsum("bi,aicxyz->abcxyz", line, core, precision=highest)
    rate = rate + jnp.einsum("ci,abixyz->abcxyz", line, core, precision=highest)
    return -kcore * rate


def heat_source(acore, shape, anchor, step_forward, extent):
    length, width, height = extent
    xterm = node_terms(
        anchor[0], shape[3], length * 0.5 + step_forward * length / 16.0, length / 8.0, length / 4.0
    )
    yterm = node_terms(anchor[1], shape[4], width * 0.5, width / 4.0, width / 4.0)
    zterm = node_terms(anchor[2], shape[5], height * 0.75, height / 8.0, height / 8.0)
    total = (
        xterm[:, None, None, :, None, None]
        + yterm[None, :, None, None, :, None]
        + zterm[None, None, :, None, None, :]
    )
    return heat_power * (2.0 / 3.0) * jnp.exp(total) * acore


def faces_length(planes):
    return with_halo(planes, (("gx", 2),), 1)


def faces_width(planes):
    return with_halo(planes, (("gy", 3),), 1)


def faces_height(planes):
    return with_halo(planes, (("gz", 4),), 1)


def advance_faces(core, diffusivity, mask, absorb_heat, anchor, step_forward, extent):
    kcore = window(diffusivity, 0, 0, 0)
    mcore = window(mask, 0, 0, 0)
    acore = window(absorb_heat, 0, 0, 0)
    rate = volume_rate(core, kcore)
    senders = (faces_length, faces_width, faces_height)
    for axis in range(3):
        bottom = jnp.take(core, 0, axis=axis)
        top = jnp.take(core, 2, axis=axis)
        edge = 2 + axis
        count = bottom.shape[edge]
        outgoing = jnp.concatenate(
            [
                lax.slice_in_dim(bottom, 0, 1, axis=edge),
                lax.slice_in_dim(top, count - 1, count, axis=edge),
            ],
            axis=edge,
        )
        received = senders[axis](outgoing)
        from_lower = lax.slice_in_dim(received, 0, 1, axis=edge)
        from_upper = lax.slice_in_dim(received, 3, 4, axis=edge)
        after = jnp.concatenate(
            [lax.slice_in_dim(bottom, 1, count, axis=edge), from_upper], axis=edge
        )
        before = jnp.concatenate(
            [from_lower, lax.slice_in_dim(top, 0, count - 1, axis=edge)], axis=edge
        )
        for offset, own, plane in ((1, 2, after), (-1, 0, before)):
            kbeside = window(diffusivity, 0, axis, offset)
            mbeside = window(mask, 0, axis, offset)
            couple = (
                penalty
                * 2.0
                * kcore
                * kbeside
                / jnp.maximum(kcore + kbeside, 1.0)
                * mcore
                * mbeside
            )
            jump = jnp.take(core, own, axis=axis) - plane
            flux = couple * jump / float(nodal_weights[own])
            rate = rate.at[(slice(None),) * axis + (own,)].add(-flux)
    source = heat_source(acore, core.shape, anchor, step_forward, extent)
    return core + time_step * mcore * (rate + source)


def gauss_point_change(change):
    table = jnp.asarray(gauss_values())
    value = jnp.einsum("pa,abcxyz->pbcxyz", table, change, precision=highest)
    value = jnp.einsum("qb,pbcxyz->pqcxyz", table, value, precision=highest)
    value = jnp.einsum("rc,pqcxyz->pqrxyz", table, value, precision=highest)
    return value


def mechanics(deformation_change, earlier_tension_state, plastic_onset_threshold, thermal):
    normal_component = deformation_change[0:3] - expansion * thermal[None]
    volume = normal_component[0] + normal_component[1] + normal_component[2]
    trial_normal = (
        earlier_tension_state[0:3]
        + lame_first * volume[None]
        + 2.0 * shear_modulus * normal_component
    )
    trial_shear = earlier_tension_state[3:6] + 2.0 * shear_modulus * deformation_change[3:6]
    pressure = (trial_normal[0] + trial_normal[1] + trial_normal[2]) / 3.0
    dev_normal = trial_normal - pressure[None]
    squares = jnp.sum(dev_normal * dev_normal, axis=0) + 2.0 * jnp.sum(
        trial_shear * trial_shear, axis=0
    )
    equivalent = jnp.sqrt(1.5 * squares)
    limit = plastic_onset_threshold[None, :]
    plastic = jnp.maximum(equivalent - limit, 0.0) / (3.0 * shear_modulus + hardening)
    factor = 1.0 - 3.0 * shear_modulus * plastic / jnp.maximum(equivalent, limit)
    new_normal = pressure[None] + factor[None] * dev_normal
    new_shear = factor[None] * trial_shear
    stress_new = jnp.concatenate([new_normal, new_shear], axis=0)
    rows = [[0, 5, 4], [5, 1, 3], [4, 3, 2]]
    tensor = jnp.stack([jnp.stack([stress_new[k] for k in row], axis=0) for row in rows], axis=0)
    forces = jnp.einsum("dig,cdgm->cim", jnp.asarray(gradient_table()), tensor, precision=highest)
    return (stress_new, forces)


def local(
    nodal_warmth_degrees,
    thermal_transfer_coefficient,
    taken_beam_fraction,
    laid_tiers,
    holding_brick_column,
    piece_onto_solid_brick,
    deformation_change,
    earlier_tension_state,
    plastic_onset_threshold,
):
    size_x, size_y, size_z = thermal_transfer_coefficient.shape
    extent = (
        size_x * lax.axis_size("gx"),
        size_y * lax.axis_size("gy"),
        size_z * lax.axis_size("gz"),
    )
    start_x = lax.axis_index("gx") * size_x
    start_y = lax.axis_index("gy") * size_y
    start_z = lax.axis_index("gz") * size_z
    mask = (jnp.arange(size_z)[None, None, :] < laid_tiers[0, 0, 0]).astype(jnp.float32)
    mask = jnp.broadcast_to(mask, thermal_transfer_coefficient.shape)
    depth = 1
    diffusivity, masked_values, absorb_heat = (
        with_halo(thermal_transfer_coefficient, (("gx", 0), ("gy", 1), ("gz", 2)), depth),
        with_halo(mask, (("gx", 0), ("gy", 1), ("gz", 2)), depth),
        with_halo(taken_beam_fraction, (("gx", 0), ("gy", 1), ("gz", 2)), depth),
    )
    nodal_quantity_entries = nodal_warmth_degrees
    for step_forward in range(STEPS):
        nodal_quantity_entries = advance_faces(
            nodal_quantity_entries,
            diffusivity,
            masked_values,
            absorb_heat,
            (start_x, start_y, start_z),
            step_forward,
            extent,
        )
    mesh_piece_sequence = size_x * size_y * size_z
    change_amount_entry = gauss_point_change(nodal_quantity_entries - nodal_warmth_degrees).reshape(
        8, mesh_piece_sequence
    )
    weights = mask.reshape(mesh_piece_sequence)
    target_owner = holding_brick_column.reshape(mesh_piece_sequence)
    target_cell = piece_onto_solid_brick.reshape(mesh_piece_sequence)
    owners = lax.axis_size("gx")
    cells = deformation_change.shape[2]
    capacity = 2 * mesh_piece_sequence // owners
    hits = (target_owner[:, None] == jnp.arange(owners)[None, :]).astype(jnp.int32)
    running = jnp.cumsum(hits, axis=0)
    position = jnp.take_along_axis(running, target_owner[:, None], axis=1)[:, 0] - 1
    labels = jnp.where(weights > 0.0, target_cell, cells)
    send_values = (
        jnp.zeros((owners, 8, capacity), jnp.float32)
        .at[target_owner, :, position]
        .set(change_amount_entry.T)
    )
    send_labels = (
        jnp.full((owners, capacity), cells, jnp.int32).at[target_owner, position].set(labels)
    )
    got_values, got_labels = (
        lax.all_to_all(send_values, "gx", split_axis=0, concat_axis=0, tiled=True),
        lax.all_to_all(send_labels, "gx", split_axis=0, concat_axis=0, tiled=True),
    )
    flat_values = jnp.transpose(got_values, (1, 0, 2)).reshape(8, owners * capacity)
    flat_labels = got_labels.reshape(owners * capacity)
    sums = jnp.zeros((8, cells + 1), jnp.float32).at[:, flat_labels].add(flat_values)[:, :cells]
    counts = jnp.zeros((cells + 1,), jnp.float32).at[flat_labels].add(1.0)[:cells]
    thermal = sums / jnp.maximum(counts, 1.0)[None, :]
    stress_new, forces = mechanics(
        deformation_change, earlier_tension_state, plastic_onset_threshold, thermal
    )
    return (nodal_quantity_entries, stress_new, forces)


def solution(mesh):
    placed = (
        P(None, None, None, "gx", "gy", "gz"),
        P("gx", "gy", "gz"),
        P("gx", "gy", "gz"),
        P("gx", "gy", "gz"),
        P("gx", "gy", "gz", None, None),
        P("gx", "gy", "gz", None),
        P(None, None, ("gx", "gy", "gz")),
        P(None, None, ("gx", "gy", "gz")),
        P(("gx", "gy", "gz")),
    )
    return jax.shard_map(
        local,
        mesh=mesh,
        in_specs=placed,
        out_specs=(
            P(None, None, None, "gx", "gy", "gz"),
            P(None, None, ("gx", "gy", "gz")),
            P(None, None, ("gx", "gy", "gz")),
        ),
        check_vma=False,
    )
```

profile of v0, /device:TPU:10, one launch (start us, length us, event | category | flops | bytes accessed | tf_op | source)
XLA Modules:
  0.0 243.1 jit_solution(14235714780832392466)
XLA Ops:
  1.3 2.4 collective-permute-start.1
  3.7 3.5 %collective-permute-start.4 = (f32[1,4,128]{2,1,0:T(4,128)S(1)}, f32[1,4,128]{2,1,0:T(4,128)S(1)}, u32[]{:S(2)}, u32[]{:S(2)}) collective-permute-start(f32[1,4,128]{2,1,0:T(4,128)S(1)} %slice.1222), channel_id=1, source_target_pairs={{0,8},{8,16},{16,24},{1,9},{9,17},{17,25},{2,10},{10,18},{18,26},{... | collective-permute-start | bytes 6152 | tf_op jit(solution)/shard_map/ppermute | solution.py:31
  7.9 3.5 %collective-permute-start.3 = (f32[1,4,128]{2,1,0:T(4,128)S(1)}, f32[1,4,128]{2,1,0:T(4,128)S(1)}, u32[]{:S(2)}, u32[]{:S(2)}) collective-permute-start(f32[1,4,128]{2,1,0:T(4,128)S(1)} %get-tuple-element.438), channel_id=1, source_target_pairs={{0,8},{8,16},{16,24},{1,9},{9,17},{17,25},{2,10},{10,18},{18,26},{... | collective-permute-start | bytes 6152 | tf_op jit(solution)/shard_map/ppermute | solution.py:31
  11.3 2.4 collective-permute-start
  19.8 17.6 %gather_fusion = s32[2048]{0:T(1024)S(1)} fusion(s32[2048,4]{0,1:T(4,128)S(1)} %bitcast.391, s32[2048]{0:T(1024)S(1)} %bitcast.392), kind=kCustom, calls=%fused_computation | custom fusion | bytes 32768 | tf_op jit(solution)/shard_map/jit(take_along_axis)/gather | solution.py:262
  37.7 8.6 %scatter_custom_fusion.2 = s32[4096]{0:T(1024)} fusion(s32[2048]{0:T(1024)S(1)} %get-tuple-element.453, s32[2048]{0:T(1024)S(1)} %get-tuple-element.454, s32[]{:T(128)} %constant.741.clone.1), kind=kCustom, calls=%fused_computation.363 | custom fusion | bytes 16388
  46.3 5.8 %all-to-all-start = ((s32[4,1,1024]{2,1,0:T(1,128)}), s32[4,1,1024]{2,1,0:T(1,128)S(1)}, u32[]{:S(2)}, u32[]{:S(2)}) async-start(s32[4,1,1024]{2,1,0:T(1,128)} %bitcast.76), calls=%async_computation | async-start | bytes 32768 | tf_op jit(solution)/shard_map/all_to_all | solution.py:274
  59.1 4.5 %collective-permute-start.9 = (f32[6,1,128]{2,1,0:T(1,128)S(1)}, f32[6,1,128]{2,1,0:T(1,128)S(1)}, u32[]{:S(2)}, u32[]{:S(2)}) collective-permute-start(f32[6,1,128]{2,1,0:T(1,128)S(1)} %get-tuple-element.423), channel_id=1, source_target_pairs={{0,4},{1,5},{2,6},{3,7},{8,12},{9,13},{10,14},{11,15},{16,20},{17,... | collective-permute-start | bytes 9224 | tf_op jit(solution)/shard_map/ppermute | solution.py:31
  66.4 2.1 collective-permute-start.15
  72.5 3.6 %collective-permute-start.12 = (f32[6,6,1]{2,1,0:T(8,128)S(1)}, f32[6,6,1]{2,1,0:T(8,128)S(1)}, u32[]{:S(2)}, u32[]{:S(2)}) collective-permute-start(f32[6,6,1]{2,1,0:T(8,128)S(1)} %get-tuple-element.418), channel_id=1, source_target_pairs={{1,0},{2,1},{3,2},{5,4},{6,5},{7,6},{9,8},{10,9},{11,10},{13,12},{... | collective-permute-start | bytes 440 | tf_op jit(solution)/shard_map/ppermute | solution.py:33
  78.4 3.4 %collective-permute-start.5 = (f32[3,3,1,4,128]{4,3,2,1,0:T(4,128)S(1)}, f32[3,3,1,4,128]{4,3,2,1,0:T(4,128)S(1)}, u32[]{:S(2)}, u32[]{:S(2)}) collective-permute-start(f32[3,3,1,4,128]{4,3,2,1,0:T(4,128)S(1)} %slice.1478), channel_id=1, source_target_pairs={{0,8},{8,16},{16,24},{1,9},{9,17},{17,25},{2,10},{10,18},{18,26},{... | collective-permute-start | bytes 55304 | tf_op jit(solution)/shard_map/ppermute | solution.py:31
  82.0 2.1 collective-permute-done.5
  84.3 2.9 %collective-permute-start.11 = (f32[3,3,4,1,128]{4,3,2,1,0:T(1,128)S(1)}, f32[3,3,4,1,128]{4,3,2,1,0:T(1,128)S(1)}, u32[]{:S(2)}, u32[]{:S(2)}) collective-permute-start(f32[3,3,4,1,128]{4,3,2,1,0:T(1,128)S(1)} %slice.1486), channel_id=1, source_target_pairs={{0,4},{1,5},{2,6},{3,7},{8,12},{9,13},{10,14},{11,15},{16,20},{17,... | collective-permute-start | bytes 55304 | tf_op jit(solution)/shard_map/ppermute | solution.py:31
  91.0 28.8 %scatter_custom_fusion.1 = f32[257]{0:T(512)S(1)} fusion(s32[4096]{0:T(1024)S(1)} %bitcast.416, f32[4096]{0:T(1024)S(1)} %broadcast.1109, f32[]{:T(128)} %constant.719.clone.1), kind=kCustom, calls=%fused_computation.403 | custom fusion | flops 4096 | bytes 1032 | tf_op jit(solution)/shard_map/scatter-add | solution.py:279
  124.5 3.6 %collective-permute-done.18 = f32[3,3,1,4,128]{4,3,2,1,0:T(4,128)S(1)} collective-permute-done((f32[3,3,1,4,128]{4,3,2,1,0:T(4,128)S(1)}, f32[3,3,1,4,128]{4,3,2,1,0:T(4,128)S(1)}, u32[]{:S(2)}, u32[]{:S(2)}) %collective-permute-start.18) | collective-permute-done | bytes 18464 | tf_op jit(solution)/shard_map/ppermute | solution.py:33
  128.1 3.4 %collective-permute-start.19 = (f32[3,3,1,4,128]{4,3,2,1,0:T(4,128)S(1)}, f32[3,3,1,4,128]{4,3,2,1,0:T(4,128)S(1)}, u32[]{:S(2)}, u32[]{:S(2)}) collective-permute-start(f32[3,3,1,4,128]{4,3,2,1,0:T(4,128)S(1)} %slice.1504), channel_id=1, source_target_pairs={{0,8},{8,16},{16,24},{1,9},{9,17},{17,25},{2,10},{10,18},{18,26},{... | collective-permute-start | bytes 55304 | tf_op jit(solution)/shard_map/ppermute | solution.py:31
  132.9 4.5 %collective-permute-start.21 = (f32[3,3,4,1,128]{4,3,2,0,1:T(1,128)S(1)}, f32[3,3,4,1,128]{4,3,2,0,1:T(1,128)S(1)}, u32[]{:S(2)}, u32[]{:S(2)}) collective-permute-start(f32[3,3,4,1,128]{4,3,2,0,1:T(1,128)S(1)} %slice.1512), channel_id=1, source_target_pairs={{0,4},{1,5},{2,6},{3,7},{8,12},{9,13},{10,14},{11,15},{16,20},{17,... | collective-permute-start | bytes 55304 | tf_op jit(solution)/shard_map/ppermute | solution.py:31
  139.6 2.6 %collective-permute-start.23 = (f32[3,3,4,4,1]{4,3,2,0,1:T(4,128)S(1)}, f32[3,3,4,4,1]{4,3,2,0,1:T(4,128)S(1)}, u32[]{:S(2)}, u32[]{:S(2)}) collective-permute-start(f32[3,3,4,4,1]{4,3,2,0,1:T(4,128)S(1)} %slice.1520), channel_id=1, source_target_pairs={{0,1},{1,2},{2,3},{4,5},{5,6},{6,7},{8,9},{9,10},{10,11},{12,13},{... | collective-permute-start | bytes 1736 | tf_op jit(solution)/shard_map/ppermute | solution.py:31
  142.7 2.6 %collective-permute-done.23 = f32[3,3,4,4,1]{4,3,2,0,1:T(4,128)S(1)} collective-permute-done((f32[3,3,4,4,1]{4,3,2,0,1:T(4,128)S(1)}, f32[3,3,4,4,1]{4,3,2,0,1:T(4,128)S(1)}, u32[]{:S(2)}, u32[]{:S(2)}) %collective-permute-start.23) | collective-permute-done | bytes 608 | tf_op jit(solution)/shard_map/ppermute | solution.py:31
  147.6 2.5 %collective-permute-start.24 = (f32[3,3,1,4,128]{4,3,2,1,0:T(4,128)S(1)}, f32[3,3,1,4,128]{4,3,2,1,0:T(4,128)S(1)}, u32[]{:S(2)}, u32[]{:S(2)}) collective-permute-start(f32[3,3,1,4,128]{4,3,2,1,0:T(4,128)S(1)} %slice.1526), channel_id=1, source_target_pairs={{8,0},{16,8},{24,16},{9,1},{17,9},{25,17},{10,2},{18,10},{26,18},{... | collective-permute-start | bytes 55304 | tf_op jit(solution)/shard_map/ppermute | solution.py:33
  150.2 3.0 %collective-permute-done.24 = f32[3,3,1,4,128]{4,3,2,1,0:T(4,128)S(1)} collective-permute-done((f32[3,3,1,4,128]{4,3,2,1,0:T(4,128)S(1)}, f32[3,3,1,4,128]{4,3,2,1,0:T(4,128)S(1)}, u32[]{:S(2)}, u32[]{:S(2)}) %collective-permute-start.24) | collective-permute-done | bytes 18464 | tf_op jit(solution)/shard_map/ppermute | solution.py:33
  156.7 4.5 %collective-permute-start.27 = (f32[3,3,4,1,128]{4,3,2,1,0:T(1,128)S(1)}, f32[3,3,4,1,128]{4,3,2,1,0:T(1,128)S(1)}, u32[]{:S(2)}, u32[]{:S(2)}) collective-permute-start(f32[3,3,4,1,128]{4,3,2,1,0:T(1,128)S(1)} %slice.1536), channel_id=1, source_target_pairs={{0,4},{1,5},{2,6},{3,7},{8,12},{9,13},{10,14},{11,15},{16,20},{17,... | collective-permute-start | bytes 55304 | tf_op jit(solution)/shard_map/ppermute | solution.py:31
  163.3 2.4 collective-permute-start.29
  166.2 2.8 %collective-permute-done.29 = f32[3,3,4,4,1]{4,3,2,1,0:T(4,128)S(1)} collective-permute-done((f32[3,3,4,4,1]{4,3,2,1,0:T(4,128)S(1)}, f32[3,3,4,4,1]{4,3,2,1,0:T(4,128)S(1)}, u32[]{:S(2)}, u32[]{:S(2)}) %collective-permute-start.29) | collective-permute-done | bytes 608 | tf_op jit(solution)/shard_map/ppermute | solution.py:31
  171.3 3.9 %collective-permute-start.30 = (f32[3,3,1,4,128]{4,3,2,1,0:T(4,128)S(1)}, f32[3,3,1,4,128]{4,3,2,1,0:T(4,128)S(1)}, u32[]{:S(2)}, u32[]{:S(2)}) collective-permute-start(f32[3,3,1,4,128]{4,3,2,1,0:T(4,128)S(1)} %slice.1550), channel_id=1, source_target_pairs={{8,0},{16,8},{24,16},{9,1},{17,9},{25,17},{10,2},{18,10},{26,18},{... | collective-permute-start | bytes 55304 | tf_op jit(solution)/shard_map/ppermute | solution.py:33
  180.4 2.3 collective-permute-done.31
  188.6 2.4 collective-permute-start.35
  191.3 3.0 %collective-permute-done.35 = f32[3,3,4,4,1]{4,3,2,1,0:T(4,128)S(1)} collective-permute-done((f32[3,3,4,4,1]{4,3,2,1,0:T(4,128)S(1)}, f32[3,3,4,4,1]{4,3,2,1,0:T(4,128)S(1)}, u32[]{:S(2)}, u32[]{:S(2)}) %collective-permute-start.35) | collective-permute-done | bytes 608 | tf_op jit(solution)/shard_map/ppermute | solution.py:31
  197.3 6.1 %scatter_custom_fusion.3 = f32[4096,8]{1,0:T(8,128)S(1)} fusion(s32[2048]{0:T(1024)S(1)} %get-tuple-element.453, f32[2048,8]{1,0:T(8,128)S(1)} %copy.489, f32[]{:T(128)} %constant.719.clone.1), kind=kCustom, calls=%fused_computation.8 | custom fusion | bytes 131076
  204.6 5.4 %all-to-all-start.1 = ((f32[4,8,1024]{2,1,0:T(8,128)}), f32[4,8,1024]{2,1,0:T(8,128)S(1)}, u32[]{:S(2)}, u32[]{:S(2)}) async-start(f32[4,8,1024]{2,1,0:T(8,128)} %bitcast.85), calls=%async_computation.1 | async-start | bytes 262144 | tf_op jit(solution)/shard_map/all_to_all | solution.py:273
  210.1 5.2 %all-to-all-done.1 = f32[4,8,1024]{2,1,0:T(8,128)S(1)} async-done(((f32[4,8,1024]{2,1,0:T(8,128)}), f32[4,8,1024]{2,1,0:T(8,128)S(1)}, u32[]{:S(2)}, u32[]{:S(2)}) %all-to-all-start.1) | async-done | bytes 131104 | tf_op jit(solution)/shard_map/all_to_all | solution.py:273
  215.8 25.5 %scatter_custom_fusion = f32[8,257]{0,1:T(8,128)S(1)} fusion(s32[4096]{0:T(1024)S(1)} %bitcast.417, f32[4096,8]{1,0:T(8,128)S(1)} %copy.491, f32[]{:T(128)} %constant.719.clone.1), kind=kCustom, calls=%fused_computation.273 | custom fusion | flops 32768 | bytes 8228 | tf_op jit(solution)/shard_map/scatter-add | solution.py:278
  (242 shorter events, 63.5 us)
Async XLA Ops:
  1.3 54.5 %collective-permute-start.1 = (f32[1,4,128]{2,1,0:T(4,128)S(1)}, f32[1,4,128]{2,1,0:T(4,128)S(1)}, u32[]{:S(2)}, u32[]{:S(2)}) collective-permute-start(f32[1,4,128]{2,1,0:T(4,128)S(1)} %slice.1222), channel_id=1, source_target_pairs={{8,0},{16,8},{24,16},{9,1},{17,9},{25,17},{10,2},{18,10},{26,18},{... | collective-permute-start | bytes 6152 | tf_op jit(solution)/shard_map/ppermute | solution.py:33
  3.7 54.1 %collective-permute-start.4 = (f32[1,4,128]{2,1,0:T(4,128)S(1)}, f32[1,4,128]{2,1,0:T(4,128)S(1)}, u32[]{:S(2)}, u32[]{:S(2)}) collective-permute-start(f32[1,4,128]{2,1,0:T(4,128)S(1)} %slice.1222), channel_id=1, source_target_pairs={{0,8},{8,16},{16,24},{1,9},{9,17},{17,25},{2,10},{10,18},{18,26},{... | collective-permute-start | bytes 6152 | tf_op jit(solution)/shard_map/ppermute | solution.py:31
  7.9 46.6 %collective-permute-start.3 = (f32[1,4,128]{2,1,0:T(4,128)S(1)}, f32[1,4,128]{2,1,0:T(4,128)S(1)}, u32[]{:S(2)}, u32[]{:S(2)}) collective-permute-start(f32[1,4,128]{2,1,0:T(4,128)S(1)} %get-tuple-element.438), channel_id=1, source_target_pairs={{0,8},{8,16},{16,24},{1,9},{9,17},{17,25},{2,10},{10,18},{18,26},{... | collective-permute-start | bytes 6152 | tf_op jit(solution)/shard_map/ppermute | solution.py:31
  11.3 46.4 %collective-permute-start = (f32[1,4,128]{2,1,0:T(4,128)S(1)}, f32[1,4,128]{2,1,0:T(4,128)S(1)}, u32[]{:S(2)}, u32[]{:S(2)}) collective-permute-start(f32[1,4,128]{2,1,0:T(4,128)S(1)} %get-tuple-element.439), channel_id=1, source_target_pairs={{8,0},{16,8},{24,16},{9,1},{17,9},{25,17},{10,2},{18,10},{26,18},{... | collective-permute-start | bytes 6152 | tf_op jit(solution)/shard_map/ppermute | solution.py:33
  14.6 63.8 %collective-permute-start.2 = (f32[3,3,1,4,128]{4,3,2,1,0:T(4,128)S(1)}, f32[3,3,1,4,128]{4,3,2,1,0:T(4,128)S(1)}, u32[]{:S(2)}, u32[]{:S(2)}) collective-permute-start(f32[3,3,1,4,128]{4,3,2,1,0:T(4,128)S(1)} %slice.1476), channel_id=1, source_target_pairs={{8,0},{16,8},{24,16},{9,1},{17,9},{25,17},{10,2},{18,10},{26,18},{... | collective-permute-start | bytes 55304 | tf_op jit(solution)/shard_map/ppermute | solution.py:33
  46.3 44.6 %all-to-all-start = ((s32[4,1,1024]{2,1,0:T(1,128)}), s32[4,1,1024]{2,1,0:T(1,128)S(1)}, u32[]{:S(2)}, u32[]{:S(2)}) async-start(s32[4,1,1024]{2,1,0:T(1,128)} %bitcast.76), calls=%async_computation | async-start | bytes 32768 | tf_op jit(solution)/shard_map/all_to_all | solution.py:274
  54.5 29.7 %collective-permute-start.8 = (f32[3,3,4,1,128]{4,3,2,1,0:T(1,128)S(1)}, f32[3,3,4,1,128]{4,3,2,1,0:T(1,128)S(1)}, u32[]{:S(2)}, u32[]{:S(2)}) collective-permute-start(f32[3,3,4,1,128]{4,3,2,1,0:T(1,128)S(1)} %slice.1483), channel_id=1, source_target_pairs={{4,0},{5,1},{6,2},{7,3},{12,8},{13,9},{14,10},{15,11},{20,16},{21,... | collective-permute-start | bytes 55304 | tf_op jit(solution)/shard_map/ppermute | solution.py:33
  55.8 32.9 %collective-permute-start.14 = (f32[3,3,4,4,1]{4,3,2,1,0:T(4,128)S(1)}, f32[3,3,4,4,1]{4,3,2,1,0:T(4,128)S(1)}, u32[]{:S(2)}, u32[]{:S(2)}) collective-permute-start(f32[3,3,4,4,1]{4,3,2,1,0:T(4,128)S(1)} %bitcast.406), channel_id=1, source_target_pairs={{1,0},{2,1},{3,2},{5,4},{6,5},{7,6},{9,8},{10,9},{11,10},{13,12},{... | collective-permute-start | bytes 1736 | tf_op jit(solution)/shard_map/ppermute | solution.py:33
  57.8 5.9 %collective-permute-start.6 = (f32[6,1,128]{2,1,0:T(1,128)S(1)}, f32[6,1,128]{2,1,0:T(1,128)S(1)}, u32[]{:S(2)}, u32[]{:S(2)}) collective-permute-start(f32[6,1,128]{2,1,0:T(1,128)S(1)} %get-tuple-element.424), channel_id=1, source_target_pairs={{4,0},{5,1},{6,2},{7,3},{12,8},{13,9},{14,10},{15,11},{20,16},{21,... | collective-permute-start | bytes 9224 | tf_op jit(solution)/shard_map/ppermute | solution.py:33
  59.1 5.9 %collective-permute-start.9 = (f32[6,1,128]{2,1,0:T(1,128)S(1)}, f32[6,1,128]{2,1,0:T(1,128)S(1)}, u32[]{:S(2)}, u32[]{:S(2)}) collective-permute-start(f32[6,1,128]{2,1,0:T(1,128)S(1)} %get-tuple-element.423), channel_id=1, source_target_pairs={{0,4},{1,5},{2,6},{3,7},{8,12},{9,13},{10,14},{11,15},{16,20},{17,... | collective-permute-start | bytes 9224 | tf_op jit(solution)/shard_map/ppermute | solution.py:31
  66.4 6.1 %collective-permute-start.15 = (f32[6,6,1]{2,1,0:T(8,128)S(1)}, f32[6,6,1]{2,1,0:T(8,128)S(1)}, u32[]{:S(2)}, u32[]{:S(2)}) collective-permute-start(f32[6,6,1]{2,1,0:T(8,128)S(1)} %get-tuple-element.417), channel_id=1, source_target_pairs={{0,1},{1,2},{2,3},{4,5},{5,6},{6,7},{8,9},{9,10},{10,11},{12,13},{... | collective-permute-start | bytes 440 | tf_op jit(solution)/shard_map/ppermute | solution.py:31
  70.6 5.6 %collective-permute-start.16 = (f32[6,6,1]{2,1,0:T(8,128)S(1)}, f32[6,6,1]{2,1,0:T(8,128)S(1)}, u32[]{:S(2)}, u32[]{:S(2)}) collective-permute-start(f32[6,6,1]{2,1,0:T(8,128)S(1)} %get-tuple-element.419), channel_id=1, source_target_pairs={{0,1},{1,2},{2,3},{4,5},{5,6},{6,7},{8,9},{9,10},{10,11},{12,13},{... | collective-permute-start | bytes 440 | tf_op jit(solution)/shard_map/ppermute | solution.py:31
  72.5 9.3 %collective-permute-start.12 = (f32[6,6,1]{2,1,0:T(8,128)S(1)}, f32[6,6,1]{2,1,0:T(8,128)S(1)}, u32[]{:S(2)}, u32[]{:S(2)}) collective-permute-start(f32[6,6,1]{2,1,0:T(8,128)S(1)} %get-tuple-element.418), channel_id=1, source_target_pairs={{1,0},{2,1},{3,2},{5,4},{6,5},{7,6},{9,8},{10,9},{11,10},{13,12},{... | collective-permute-start | bytes 440 | tf_op jit(solution)/shard_map/ppermute | solution.py:33
  76.2 5.6 %collective-permute-start.13 = (f32[6,6,1]{2,1,0:T(8,128)S(1)}, f32[6,6,1]{2,1,0:T(8,128)S(1)}, u32[]{:S(2)}, u32[]{:S(2)}) collective-permute-start(f32[6,6,1]{2,1,0:T(8,128)S(1)} %get-tuple-element.420), channel_id=1, source_target_pairs={{1,0},{2,1},{3,2},{5,4},{6,5},{7,6},{9,8},{10,9},{11,10},{13,12},{... | collective-permute-start | bytes 440 | tf_op jit(solution)/shard_map/ppermute | solution.py:33
  78.4 5.7 %collective-permute-start.5 = (f32[3,3,1,4,128]{4,3,2,1,0:T(4,128)S(1)}, f32[3,3,1,4,128]{4,3,2,1,0:T(4,128)S(1)}, u32[]{:S(2)}, u32[]{:S(2)}) collective-permute-start(f32[3,3,1,4,128]{4,3,2,1,0:T(4,128)S(1)} %slice.1478), channel_id=1, source_target_pairs={{0,8},{8,16},{16,24},{1,9},{9,17},{17,25},{2,10},{10,18},{18,26},{... | collective-permute-start | bytes 55304 | tf_op jit(solution)/shard_map/ppermute | solution.py:31
  89.0 30.8 %collective-permute-start.17 = (f32[3,3,4,4,1]{4,3,2,1,0:T(4,128)S(1)}, f32[3,3,4,4,1]{4,3,2,1,0:T(4,128)S(1)}, u32[]{:S(2)}, u32[]{:S(2)}) collective-permute-start(f32[3,3,4,4,1]{4,3,2,1,0:T(4,128)S(1)} %slice.1496), channel_id=1, source_target_pairs={{0,1},{1,2},{2,3},{4,5},{5,6},{6,7},{8,9},{9,10},{10,11},{12,13},{... | collective-permute-start | bytes 1736 | tf_op jit(solution)/shard_map/ppermute | solution.py:31
  122.4 5.7 %collective-permute-start.18 = (f32[3,3,1,4,128]{4,3,2,1,0:T(4,128)S(1)}, f32[3,3,1,4,128]{4,3,2,1,0:T(4,128)S(1)}, u32[]{:S(2)}, u32[]{:S(2)}) collective-permute-start(f32[3,3,1,4,128]{4,3,2,1,0:T(4,128)S(1)} %slice.1502), channel_id=1, source_target_pairs={{8,0},{16,8},{24,16},{9,1},{17,9},{25,17},{10,2},{18,10},{26,18},{... | collective-permute-start | bytes 55304 | tf_op jit(solution)/shard_map/ppermute | solution.py:33
  128.1 14.1 %collective-permute-start.19 = (f32[3,3,1,4,128]{4,3,2,1,0:T(4,128)S(1)}, f32[3,3,1,4,128]{4,3,2,1,0:T(4,128)S(1)}, u32[]{:S(2)}, u32[]{:S(2)}) collective-permute-start(f32[3,3,1,4,128]{4,3,2,1,0:T(4,128)S(1)} %slice.1504), channel_id=1, source_target_pairs={{0,8},{8,16},{16,24},{1,9},{9,17},{17,25},{2,10},{10,18},{18,26},{... | collective-permute-start | bytes 55304 | tf_op jit(solution)/shard_map/ppermute | solution.py:31
  131.6 10.7 %collective-permute-start.20 = (f32[3,3,4,1,128]{4,3,2,0,1:T(1,128)S(1)}, f32[3,3,4,1,128]{4,3,2,0,1:T(1,128)S(1)}, u32[]{:S(2)}, u32[]{:S(2)}) collective-permute-start(f32[3,3,4,1,128]{4,3,2,0,1:T(1,128)S(1)} %slice.1510), channel_id=1, source_target_pairs={{4,0},{5,1},{6,2},{7,3},{12,8},{13,9},{14,10},{15,11},{20,16},{21,... | collective-permute-start | bytes 55304 | tf_op jit(solution)/shard_map/ppermute | solution.py:33
  132.9 9.5 %collective-permute-start.21 = (f32[3,3,4,1,128]{4,3,2,0,1:T(1,128)S(1)}, f32[3,3,4,1,128]{4,3,2,0,1:T(1,128)S(1)}, u32[]{:S(2)}, u32[]{:S(2)}) collective-permute-start(f32[3,3,4,1,128]{4,3,2,0,1:T(1,128)S(1)} %slice.1512), channel_id=1, source_target_pairs={{0,4},{1,5},{2,6},{3,7},{8,12},{9,13},{10,14},{11,15},{16,20},{17,... | collective-permute-start | bytes 55304 | tf_op jit(solution)/shard_map/ppermute | solution.py:31
  139.6 5.7 %collective-permute-start.23 = (f32[3,3,4,4,1]{4,3,2,0,1:T(4,128)S(1)}, f32[3,3,4,4,1]{4,3,2,0,1:T(4,128)S(1)}, u32[]{:S(2)}, u32[]{:S(2)}) collective-permute-start(f32[3,3,4,4,1]{4,3,2,0,1:T(4,128)S(1)} %slice.1520), channel_id=1, source_target_pairs={{0,1},{1,2},{2,3},{4,5},{5,6},{6,7},{8,9},{9,10},{10,11},{12,13},{... | collective-permute-start | bytes 1736 | tf_op jit(solution)/shard_map/ppermute | solution.py:31
  147.6 5.7 %collective-permute-start.24 = (f32[3,3,1,4,128]{4,3,2,1,0:T(4,128)S(1)}, f32[3,3,1,4,128]{4,3,2,1,0:T(4,128)S(1)}, u32[]{:S(2)}, u32[]{:S(2)}) collective-permute-start(f32[3,3,1,4,128]{4,3,2,1,0:T(4,128)S(1)} %slice.1526), channel_id=1, source_target_pairs={{8,0},{16,8},{24,16},{9,1},{17,9},{25,17},{10,2},{18,10},{26,18},{... | collective-permute-start | bytes 55304 | tf_op jit(solution)/shard_map/ppermute | solution.py:33
  153.3 12.5 %collective-permute-start.25 = (f32[3,3,1,4,128]{4,3,2,1,0:T(4,128)S(1)}, f32[3,3,1,4,128]{4,3,2,1,0:T(4,128)S(1)}, u32[]{:S(2)}, u32[]{:S(2)}) collective-permute-start(f32[3,3,1,4,128]{4,3,2,1,0:T(4,128)S(1)} %slice.1528), channel_id=1, source_target_pairs={{0,8},{8,16},{16,24},{1,9},{9,17},{17,25},{2,10},{10,18},{18,26},{... | collective-permute-start | bytes 55304 | tf_op jit(solution)/shard_map/ppermute | solution.py:31
  155.3 10.5 %collective-permute-start.26 = (f32[3,3,4,1,128]{4,3,2,1,0:T(1,128)S(1)}, f32[3,3,4,1,128]{4,3,2,1,0:T(1,128)S(1)}, u32[]{:S(2)}, u32[]{:S(2)}) collective-permute-start(f32[3,3,4,1,128]{4,3,2,1,0:T(1,128)S(1)} %copy.508), channel_id=1, source_target_pairs={{4,0},{5,1},{6,2},{7,3},{12,8},{13,9},{14,10},{15,11},{20,16},{21,... | collective-permute-start | bytes 55304 | tf_op jit(solution)/shard_map/ppermute | solution.py:33
  156.7 9.3 %collective-permute-start.27 = (f32[3,3,4,1,128]{4,3,2,1,0:T(1,128)S(1)}, f32[3,3,4,1,128]{4,3,2,1,0:T(1,128)S(1)}, u32[]{:S(2)}, u32[]{:S(2)}) collective-permute-start(f32[3,3,4,1,128]{4,3,2,1,0:T(1,128)S(1)} %slice.1536), channel_id=1, source_target_pairs={{0,4},{1,5},{2,6},{3,7},{8,12},{9,13},{10,14},{11,15},{16,20},{17,... | collective-permute-start | bytes 55304 | tf_op jit(solution)/shard_map/ppermute | solution.py:31
  163.3 5.7 %collective-permute-start.29 = (f32[3,3,4,4,1]{4,3,2,1,0:T(4,128)S(1)}, f32[3,3,4,4,1]{4,3,2,1,0:T(4,128)S(1)}, u32[]{:S(2)}, u32[]{:S(2)}) collective-permute-start(f32[3,3,4,4,1]{4,3,2,1,0:T(4,128)S(1)} %slice.1544), channel_id=1, source_target_pairs={{0,1},{1,2},{2,3},{4,5},{5,6},{6,7},{8,9},{9,10},{10,11},{12,13},{... | collective-permute-start | bytes 1736 | tf_op jit(solution)/shard_map/ppermute | solution.py:31
  171.3 5.7 %collective-permute-start.30 = (f32[3,3,1,4,128]{4,3,2,1,0:T(4,128)S(1)}, f32[3,3,1,4,128]{4,3,2,1,0:T(4,128)S(1)}, u32[]{:S(2)}, u32[]{:S(2)}) collective-permute-start(f32[3,3,1,4,128]{4,3,2,1,0:T(4,128)S(1)} %slice.1550), channel_id=1, source_target_pairs={{8,0},{16,8},{24,16},{9,1},{17,9},{25,17},{10,2},{18,10},{26,18},{... | collective-permute-start | bytes 55304 | tf_op jit(solution)/shard_map/ppermute | solution.py:33
  177.0 5.7 %collective-permute-start.31 = (f32[3,3,1,4,128]{4,3,2,1,0:T(4,128)S(1)}, f32[3,3,1,4,128]{4,3,2,1,0:T(4,128)S(1)}, u32[]{:S(2)}, u32[]{:S(2)}) collective-permute-start(f32[3,3,1,4,128]{4,3,2,1,0:T(4,128)S(1)} %slice.1552), channel_id=1, source_target_pairs={{0,8},{8,16},{16,24},{1,9},{9,17},{17,25},{2,10},{10,18},{18,26},{... | collective-permute-start | bytes 55304 | tf_op jit(solution)/shard_map/ppermute | solution.py:31
  179.0 5.7 %collective-permute-start.32 = (f32[3,3,4,1,128]{4,3,2,0,1:T(1,128)S(1)}, f32[3,3,4,1,128]{4,3,2,0,1:T(1,128)S(1)}, u32[]{:S(2)}, u32[]{:S(2)}) collective-permute-start(f32[3,3,4,1,128]{4,3,2,0,1:T(1,128)S(1)} %slice.1558), channel_id=1, source_target_pairs={{4,0},{5,1},{6,2},{7,3},{12,8},{13,9},{14,10},{15,11},{20,16},{21,... | collective-permute-start | bytes 55304 | tf_op jit(solution)/shard_map/ppermute | solution.py:33
  184.8 6.2 %collective-permute-start.33 = (f32[3,3,4,1,128]{4,3,2,0,1:T(1,128)S(1)}, f32[3,3,4,1,128]{4,3,2,0,1:T(1,128)S(1)}, u32[]{:S(2)}, u32[]{:S(2)}) collective-permute-start(f32[3,3,4,1,128]{4,3,2,0,1:T(1,128)S(1)} %slice.1560), channel_id=1, source_target_pairs={{0,4},{1,5},{2,6},{3,7},{8,12},{9,13},{10,14},{11,15},{16,20},{17,... | collective-permute-start | bytes 55304 | tf_op jit(solution)/shard_map/ppermute | solution.py:31
  188.6 5.7 %collective-permute-start.35 = (f32[3,3,4,4,1]{4,3,2,1,0:T(4,128)S(1)}, f32[3,3,4,4,1]{4,3,2,1,0:T(4,128)S(1)}, u32[]{:S(2)}, u32[]{:S(2)}) collective-permute-start(f32[3,3,4,4,1]{4,3,2,1,0:T(4,128)S(1)} %slice.1568), channel_id=1, source_target_pairs={{0,1},{1,2},{2,3},{4,5},{5,6},{6,7},{8,9},{9,10},{10,11},{12,13},{... | collective-permute-start | bytes 1736 | tf_op jit(solution)/shard_map/ppermute | solution.py:31
  204.6 10.6 %all-to-all-start.1 = ((f32[4,8,1024]{2,1,0:T(8,128)}), f32[4,8,1024]{2,1,0:T(8,128)S(1)}, u32[]{:S(2)}, u32[]{:S(2)}) async-start(f32[4,8,1024]{2,1,0:T(8,128)} %bitcast.85), calls=%async_computation.1 | async-start | bytes 262144 | tf_op jit(solution)/shard_map/all_to_all | solution.py:273
  (19 other events, 364.1 us)
where the time goes:
time: 245 us; the launch traced here: 243 us
  starting transfers between devices  97.4 us (40%)
  other arithmetic  63 us (26%)
  local copies, waits for them, and re-layouts  38 us (16%)
  waiting for transfers between devices  31.4 us (13%)
  matrix products  10.3 us (4%)
  between operations  2.86 us (1%)
    ppermute x18, starting transfers between devices, with_halo(): lax.ppermute(tail, axis, [(i, (i + 1) % count) for i in range(ends)])  50.3 us
    ppermute x18, starting transfers between devices, with_halo(): lax.ppermute(head, axis, [((i + 1) % count, i) for i in range(ends)])  35.9 us
    scatter-add x1, other arithmetic, local(): jnp.zeros((cells + 1,), jnp.float32).at[flat_labels].add(1.0)[:cells]  28.8 us
    scatter-add x1, other arithmetic, local(): jnp.zeros((8, cells + 1), jnp.float32).at[:, flat_labels].add(flat_values)  25.5 us
    gather x1, local copies, waits for them, and re-layouts, local(): jnp.take_along_axis(running, target_owner[:, None], axis=1)[:, 0] - 1  17.6 us
    unnamed x37, local copies, waits for them, and re-layouts  16.2 us
    ppermute x18, waiting for transfers between devices, with_halo(): lax.ppermute(tail, axis, [(i, (i + 1) % count) for i in range(ends)])  14.1 us
    ppermute x18, waiting for transfers between devices, with_halo(): lax.ppermute(head, axis, [((i + 1) % count, i) for i in range(ends)])  12.1 us
  transfers between devices with their start and end apart: 38, of which 12 were waited for; matrix products, arithmetic and copies ran while one was open for 27% of the time, Pallas kernels for 0%

commit v1 on v0

v1 whole, which is shorter than its diff:
```python
import functools
import math

import jax
import jax.numpy as jnp
from jax import lax
from jax.experimental import pallas as pl
from jax.experimental.pallas import tpu as pltpu
from jax.sharding import PartitionSpec as P

STEPS = 4

time_step = 0.003
penalty = 3.0
heat_power = 100.0
expansion = 0.02
shear_modulus = 100.0 / 2.6
lame_first = 30.0 / 0.52
hardening = 10.0
LANES = 128
GROUP = 8
MESH = pl.DeviceIdType.MESH


def face_planes(axis, side):
    planes = []
    for first in range(3):
        for second in range(3):
            index = [first, second]
            index.insert(axis, side)
            planes.append(9 * index[0] + 3 * index[1] + index[2])
    return planes


def gauss_rows():
    half = 0.5 / math.sqrt(3.0)
    return [
        [2.0 * (g - 0.5) * (g - 1.0), -4.0 * g * (g - 1.0), 2.0 * g * (g - 0.5)]
        for g in (0.5 - half, 0.5 + half)
    ]


def pair_coefficient(own, beside):
    scale = time_step * penalty * 2.0 * 6.0
    return scale * own * beside / jnp.maximum(own + beside, 1.0)


def kernel(
    block,
    counts_of,
    cells,
    tiers,
    warm_hbm,
    cond_hbm,
    beam_hbm,
    owner_hbm,
    piece_hbm,
    strain_hbm,
    stress_hbm,
    limit_hbm,
    temp_out,
    stress_out,
    forces_out,
    warm,
    cond,
    beam,
    owner,
    piece,
    strain,
    stress,
    limit,
    ping,
    pong,
    send_x,
    send_y,
    send_z,
    got_x,
    got_y,
    got_z,
    points,
    spread,
    hot,
    outbox,
    inbox,
    new_stress,
    new_forces,
    in_sems,
    out_sems,
    halo_send,
    halo_recv,
    trade_send,
    trade_recv,
):
    size_x, size_y, size_z = block
    rows = size_x * size_y
    names = ("gx", "gy", "gz")
    places = tuple(lax.axis_index(name) for name in names)
    has_lower = tuple(place > 0 for place in places)
    has_upper = tuple(place < count - 1 for place, count in zip(places, counts_of))
    peers = counts_of[0]
    chunks = cells // LANES
    slots = peers * chunks

    loads = [
        pltpu.make_async_copy(source, target, in_sems.at[index])
        for index, (source, target) in enumerate(
            (
                (warm_hbm, warm),
                (cond_hbm, cond),
                (beam_hbm, beam),
                (owner_hbm, owner),
                (piece_hbm, piece),
                (strain_hbm, strain),
                (stress_hbm, stress),
                (limit_hbm, limit),
            )
        )
    ]
    for load in loads:
        load.start()

    barrier = pltpu.get_barrier_semaphore()
    for shift in range(1, peers):
        pl.semaphore_signal(
            barrier, inc=1, device_id={"gx": lax.rem(places[0] + shift, peers)}, device_id_type=MESH
        )
    for axis in (1, 2):
        for exists, move in ((has_lower[axis], -1), (has_upper[axis], 1)):

            @pl.when(exists)
            def _(axis=axis, move=move):
                pl.semaphore_signal(
                    barrier, inc=1, device_id={names[axis]: places[axis] + move}, device_id_type=MESH
                )

    sends = (send_x, send_y, send_z)
    gots = (got_x, got_y, got_z)

    for axis in range(3):
        for exists, side in ((has_lower[axis], 0), (has_upper[axis], 1)):

            @pl.when(jnp.logical_not(exists))
            def _(axis=axis, side=side):
                gots[axis][:, side] = jnp.zeros(gots[axis].shape[:1] + gots[axis].shape[2:], jnp.float32)

    def halo(step, axis, up):
        index = (step * 3 + axis) * 2
        target = places[axis] + (1 if up else -1)
        return pltpu.make_async_remote_copy(
            src_ref=sends[axis].at[step, 1 if up else 0],
            dst_ref=gots[axis].at[step, 0 if up else 1],
            send_sem=halo_send.at[index + (1 if up else 0)],
            recv_sem=halo_recv.at[index + (0 if up else 1)],
            device_id={names[axis]: target},
            device_id_type=MESH,
        )

    lane = lax.broadcasted_iota(jnp.int32, (rows, LANES), 1)
    row = lax.broadcasted_iota(jnp.int32, (rows, LANES), 0)
    row_x = row // size_y
    row_y = row - row_x * size_y

    for load in loads[:3]:
        load.wait()
    mask = (lane < tiers[0, 0]).astype(jnp.float32)
    flow = cond[...] * mask

    send_x[0, 0, 9 * size_y : 10 * size_y] = flow[:size_y]
    send_x[0, 1, 9 * size_y : 10 * size_y] = flow[rows - size_y :]
    hold = pong
    hold[0:rows] = flow
    send_y[0, 0, 9 * size_x : 10 * size_x] = hold[pl.ds(0, size_x, stride=size_y)]
    send_y[0, 1, 9 * size_x : 10 * size_x] = hold[pl.ds(size_y - 1, size_x, stride=size_y)]

    neighbours = peers - 1
    for axis in (1, 2):
        neighbours = neighbours + has_lower[axis].astype(jnp.int32) + has_upper[axis].astype(jnp.int32)

    def pack(current, step):
        for side, face in ((0, 0), (1, 2)):
            first = 0 if side == 0 else rows - size_y
            for v, plane in enumerate(face_planes(0, face)):
                send_x[step, side, v * size_y : (v + 1) * size_y] = current[
                    plane * rows + first : plane * rows + first + size_y
                ]
            first = 0 if side == 0 else size_y - 1
            for v, plane in enumerate(face_planes(1, face)):
                send_y[step, side, v * size_x : (v + 1) * size_x] = current[
                    pl.ds(plane * rows + first, size_x, stride=size_y)
                ]
            first = 0 if side == 0 else LANES - 1
            packed = None
            for v, plane in enumerate(face_planes(2, face)):
                value = current[plane * rows : (plane + 1) * rows]
                shift = (v - first) % LANES
                value = pltpu.roll(value, shift, 1) if shift else value
                packed = value if packed is None else jnp.where(lane == v, value, packed)
            if step == 0:
                shift = (9 - first) % LANES
                packed = jnp.where(lane == 9, pltpu.roll(flow, shift, 1), packed)
            send_z[step, side] = packed

    def start(step):
        for axis in range(3):
            for up, exists in ((False, has_lower[axis]), (True, has_upper[axis])):

                @pl.when(exists)
                def _(axis=axis, up=up):
                    halo(step, axis, up).start()

    def arrive(step):
        for axis in range(3):
            for up, exists in ((False, has_upper[axis]), (True, has_lower[axis])):

                @pl.when(exists)
                def _(axis=axis, up=up):
                    halo(step, axis, up).wait_recv()

    pack(warm, 0)
    pl.semaphore_wait(barrier, neighbours)
    start(0)

    def inner(value, axis):
        if axis == 0:
            down, up = pltpu.roll(value, size_y, 0), pltpu.roll(value, rows - size_y, 0)
            low, high = row_x == 0, row_x == size_x - 1
        elif axis == 1:
            down, up = pltpu.roll(value, 1, 0), pltpu.roll(value, rows - 1, 0)
            low, high = row_y == 0, row_y == size_y - 1
        else:
            down, up = pltpu.roll(value, 1, 1), pltpu.roll(value, LANES - 1, 1)
            low, high = lane == 0, lane == LANES - 1
        return (
            jnp.where(low, 0.0, pair_coefficient(value, down)),
            jnp.where(high, 0.0, pair_coefficient(value, up)),
        )

    couples = [inner(flow, axis) for axis in range(3)]
    through = time_step * flow
    extent = [size * count for size, count in zip(block, counts_of)]
    begin = [(place * size) for place, size in zip(places, block)]

    def bell(where, node, centre, near, far):
        offset = where + 0.5 * node - centre
        ratio = offset / jnp.where(offset >= 0.0, near, far)
        return jnp.exp(-3.0 * ratio * ratio)

    where_x = (row_x + begin[0]).astype(jnp.float32)
    where_y = (row_y + begin[1]).astype(jnp.float32)
    where_z = (lane + begin[2]).astype(jnp.float32)
    length, width, height = extent
    heat = (time_step * heat_power * (2.0 / 3.0)) * mask * beam[...]
    bell_y = [bell(where_y, node, width * 0.5, width / 4.0, width / 4.0) for node in range(3)]
    bell_z = [
        heat * bell(where_z, node, height * 0.75, height / 8.0, height / 8.0) for node in range(3)
    ]

    def advance(current, following, step):
        bell_x = [
            bell(
                where_x,
                node,
                length * 0.5 + step * length / 16.0,
                length / 8.0,
                length / 4.0,
            )
            for node in range(3)
        ]
        for part in range(rows // GROUP):
            cut = slice(part * GROUP, (part + 1) * GROUP)
            t = [
                current[plane * rows + part * GROUP : plane * rows + (part + 1) * GROUP]
                for plane in range(27)
            ]
            rate = [None] * 27
            for axis in range(3):
                for v in range(9):
                    p0, p1, p2 = (face_planes(axis, k)[v] for k in range(3))
                    d0, d2 = t[p0] - t[p1], t[p2] - t[p1]
                    both = 2.0 * (d0 + d2)
                    for plane, term in (
                        (p0, both + 12.0 * d0),
                        (p1, -2.0 * both),
                        (p2, both + 12.0 * d2),
                    ):
                        rate[plane] = term if rate[plane] is None else rate[plane] + term
            for a in range(3):
                for b in range(3):
                    beam_ab = bell_x[a][cut] * bell_y[b][cut]
                    for c in range(3):
                        plane = 9 * a + 3 * b + c
                        value = t[plane] - through[cut] * rate[plane] + beam_ab * bell_z[c][cut]
                        following[plane * rows + part * GROUP : plane * rows + (part + 1) * GROUP] = value
        for axis in range(3):
            along = 1 if axis == 2 else 0
            span = LANES if axis == 2 else rows
            shift = (size_y, 1, 1)[axis]
            for p0, p2 in zip(face_planes(axis, 0), face_planes(axis, 2)):
                s0 = slice(p0 * rows, (p0 + 1) * rows)
                s2 = slice(p2 * rows, (p2 + 1) * rows)
                bottom, top = current[s0], current[s2]
                following[s0] += couples[axis][0] * (pltpu.roll(top, shift, along) - bottom)
                following[s2] += couples[axis][1] * (pltpu.roll(bottom, span - shift, along) - top)

    def fix(current, following, step, edges):
        for side, face in ((0, 0), (1, 2)):
            first = 0 if side == 0 else rows - size_y
            for v, plane in enumerate(face_planes(0, face)):
                at = slice(plane * rows + first, plane * rows + first + size_y)
                beside = got_x[step, side, v * size_y : (v + 1) * size_y]
                following[at] += edges[0][side] * (beside - current[at])
            first = 0 if side == 0 else size_y - 1
            for v, plane in enumerate(face_planes(1, face)):
                at = pl.ds(plane * rows + first, size_x, stride=size_y)
                beside = got_y[step, side, v * size_x : (v + 1) * size_x]
                following[at] = following[at] + edges[1][side] * (beside - current[at])
            first = 0 if side == 0 else LANES - 1
            packed = got_z[step, side]
            for v, plane in enumerate(face_planes(2, face)):
                at = slice(plane * rows, (plane + 1) * rows)
                shift = (first - v) % LANES
                beside = pltpu.roll(packed, shift, 1) if shift else packed
                following[at] += edges[2][side] * (beside - current[at])

    def outer_couples():
        points[0:rows] = flow
        edges = []
        edges.append(
            [
                pair_coefficient(
                    flow[first : first + size_y], got_x[0, side, 9 * size_y : 10 * size_y]
                )
                for side, first in ((0, 0), (1, rows - size_y))
            ]
        )
        edges.append(
            [
                pair_coefficient(
                    points[pl.ds(first, size_x, stride=size_y)],
                    got_y[0, side, 9 * size_x : 10 * size_x],
                )
                for side, first in ((0, 0), (1, size_y - 1))
            ]
        )
        edges.append(
            [
                jnp.where(
                    lane == first,
                    pair_coefficient(flow, pltpu.roll(got_z[0, side], (first - 9) % LANES, 1)),
                    0.0,
                )
                for side, first in ((0, 0), (1, LANES - 1))
            ]
        )
        return edges

    def label_rows():
        for load in loads[3:5]:
            load.wait()
        low_iota = lax.broadcasted_iota(jnp.int32, (LANES, LANES), 0)
        slot_iota = lax.broadcasted_iota(jnp.int32, (slots, LANES), 0)
        cell = piece[...]
        chunk = cell // LANES
        low = cell - chunk * LANES
        slot = jnp.where(lane < tiers[0, 0], owner[...] * chunks + chunk, -1)
        for r in range(rows):
            at = slice(r * LANES, (r + 1) * LANES)
            hot[:, at] = (low_iota == low[r : r + 1]).astype(jnp.float32).astype(jnp.bfloat16)
            spread[slots * 2 * GROUP :, at] = (
                (slot_iota == slot[r : r + 1]).astype(jnp.float32).astype(jnp.bfloat16)
            )
        return slot

    slot = None
    edges = None
    current = warm
    for step in range(STEPS):
        following = ping if step % 2 == 0 else pong
        if step > 0:
            pack(current, step)
            start(step)
        advance(current, following, step)
        if step == 0:
            slot = label_rows()
        arrive(step)
        if step == 0:
            edges = outer_couples()
        fix(current, following, step, edges)
        current = following

    write_temp = pltpu.make_async_copy(current, temp_out, out_sems.at[0])
    write_temp.start()

    table = gauss_rows()
    for part in range(rows // GROUP):
        change = [
            current[p * rows + part * GROUP : p * rows + (part + 1) * GROUP]
            - warm[p * rows + part * GROUP : p * rows + (part + 1) * GROUP]
            for p in range(27)
        ]
        stage = [
            [sum(table[p][a] * change[9 * a + v] for a in range(3)) for v in range(9)] for p in range(2)
        ]
        stage = [
            [
                [sum(table[q][b] * stage[p][3 * b + c] for b in range(3)) for c in range(3)]
                for q in range(2)
            ]
            for p in range(2)
        ]
        for p in range(2):
            for q in range(2):
                for r in range(2):
                    g = 4 * p + 2 * q + r
                    points[g * rows + part * GROUP : g * rows + (part + 1) * GROUP] = sum(
                        table[r][c] * stage[p][q][c] for c in range(3)
                    )

    for r in range(rows):
        at = slice(r * LANES, (r + 1) * LANES)
        value = points[pl.ds(r, GROUP, stride=rows)]
        coarse = value.astype(jnp.bfloat16).astype(jnp.float32)
        both = jnp.concatenate([coarse, value - coarse], axis=0)
        mine = jnp.broadcast_to(slot[r : r + 1], (2 * GROUP, LANES))
        for s in range(slots):
            spread[s * 2 * GROUP : (s + 1) * 2 * GROUP, at] = jnp.where(mine == s, both, 0.0).astype(
                jnp.bfloat16
            )
    total = lax.dot_general(
        spread[...], hot[...], (((1,), (1,)), ((), ())), preferred_element_type=jnp.float32
    )
    for o in range(peers):
        for k in range(chunks):
            s = o * chunks + k
            outbox[o, k * GROUP : (k + 1) * GROUP] = (
                total[s * 2 * GROUP : s * 2 * GROUP + GROUP]
                + total[s * 2 * GROUP + GROUP : (s + 1) * 2 * GROUP]
            )
        first = slots * 2 * GROUP + o * chunks
        outbox[o, chunks * GROUP :] = jnp.zeros((outbox.shape[1] - chunks * GROUP, LANES), jnp.float32)
        outbox[o, chunks * GROUP : chunks * GROUP + chunks] = total[first : first + chunks]

    trades = []
    for shift in range(1, peers):
        peer = lax.rem(places[0] + shift, peers)
        trades.append(
            pltpu.make_async_remote_copy(
                src_ref=outbox.at[peer],
                dst_ref=inbox.at[shift - 1],
                send_sem=trade_send.at[shift - 1],
                recv_sem=trade_recv.at[shift - 1],
                device_id={"gx": peer},
                device_id_type=MESH,
            )
        )
    for trade in trades:
        trade.start()
    for load in loads[5:]:
        load.wait()
    for trade in trades:
        trade.wait_recv()

    point = lax.broadcasted_iota(jnp.int32, (GROUP, LANES), 0)
    bits = [(point // size) % 2 for size in (4, 2, 1)]

    def partner(value, axis):
        size = (4, 2, 1)[axis]
        if size * 2 == GROUP:
            return pltpu.roll(value, size, 0)
        return jnp.where(
            bits[axis] == 0, pltpu.roll(value, GROUP - size, 0), pltpu.roll(value, size, 0)
        )

    near = 0.5 + 0.5 / math.sqrt(3.0)
    far = 0.5 - 0.5 / math.sqrt(3.0)
    signs = [bits[axis].astype(jnp.float32) * 2.0 - 1.0 for axis in range(3)]

    def shaped(value, axis):
        return near * value + far * partner(value, axis)

    def sloped(value, axis):
        return signs[axis] * (value + partner(value, axis))

    for k in range(chunks):
        at = slice(k * LANES, (k + 1) * LANES)
        own = pl.ds(k * GROUP, GROUP)
        sums = outbox[places[0], own]
        count = outbox[places[0], pl.ds(chunks * GROUP + k, 1)]
        for shift in range(1, peers):
            sums = sums + inbox[shift - 1, own]
            count = count + inbox[shift - 1, pl.ds(chunks * GROUP + k, 1)]
        thermal = sums / jnp.maximum(count, 1.0)
        normal = [strain[d, :, at] - expansion * thermal for d in range(3)]
        volume = normal[0] + normal[1] + normal[2]
        trial = [
            stress[d, :, at] + lame_first * volume + (2.0 * shear_modulus) * normal[d] for d in range(3)
        ]
        shear = [stress[d, :, at] + (2.0 * shear_modulus) * strain[d, :, at] for d in range(3, 6)]
        pressure = (trial[0] + trial[1] + trial[2]) / 3.0
        deviator = [value - pressure for value in trial]
        squares = (
            deviator[0] * deviator[0] + deviator[1] * deviator[1] + deviator[2] * deviator[2]
        ) + 2.0 * (shear[0] * shear[0] + shear[1] * shear[1] + shear[2] * shear[2])
        equivalent = jnp.sqrt(1.5 * squares)
        bound = limit[0:1, at]
        plastic = jnp.maximum(equivalent - bound, 0.0) / (3.0 * shear_modulus + hardening)
        factor = 1.0 - 3.0 * shear_modulus * plastic / jnp.maximum(equivalent, bound)
        result = [pressure + factor * value for value in deviator] + [factor * value for value in shear]
        for d in range(6):
            new_stress[d, :, at] = result[d]
        picks = [[0, 5, 4], [5, 1, 3], [4, 3, 2]]
        for c in range(3):
            fx, fy, fz = (result[d] * 0.125 for d in picks[c])
            plane = shaped(sloped(fx, 0) , 1) + sloped(shaped(fy, 0), 1)
            new_forces[c, :, at] = shaped(plane, 2) + sloped(shaped(shaped(fz, 0), 1), 2)

    write_stress = pltpu.make_async_copy(new_stress, stress_out, out_sems.at[1])
    write_forces = pltpu.make_async_copy(new_forces, forces_out, out_sems.at[2])
    write_stress.start()
    write_forces.start()
    for trade in trades:
        trade.wait_send()
    for step in range(STEPS):
        for axis in range(3):
            for up, exists in ((False, has_lower[axis]), (True, has_upper[axis])):

                @pl.when(exists)
                def _(step=step, axis=axis, up=up):
                    halo(step, axis, up).wait_send()

    write_temp.wait()
    write_stress.wait()
    write_forces.wait()


def local(
    counts_of,
    nodal_warmth_degrees,
    thermal_transfer_coefficient,
    taken_beam_fraction,
    laid_tiers,
    holding_brick_column,
    piece_onto_solid_brick,
    deformation_change,
    earlier_tension_state,
    plastic_onset_threshold,
):
    block = thermal_transfer_coefficient.shape
    size_x, size_y, size_z = block
    rows = size_x * size_y
    cells = deformation_change.shape[2]
    assert size_z == LANES and rows % GROUP == 0 and cells % LANES == 0
    chunks = cells // LANES
    peers = counts_of[0]
    slots = peers * chunks
    box = (chunks * GROUP + -(-chunks // GROUP) * GROUP, LANES)
    flat = (rows, LANES)
    f32 = jnp.float32
    anywhere = pl.BlockSpec(memory_space=pl.ANY)
    vmem = pltpu.VMEM
    temp, stress, forces = pl.pallas_call(
        functools.partial(kernel, block, counts_of, cells),
        out_shape=(
            jax.ShapeDtypeStruct((27 * rows, LANES), f32),
            jax.ShapeDtypeStruct(earlier_tension_state.shape, f32),
            jax.ShapeDtypeStruct((3, 8, cells), f32),
        ),
        in_specs=[pl.BlockSpec(memory_space=pltpu.SMEM)] + [anywhere] * 8,
        out_specs=(anywhere,) * 3,
        scratch_shapes=[
            vmem((27 * rows, LANES), f32),
            vmem(flat, f32),
            vmem(flat, f32),
            vmem(flat, jnp.int32),
            vmem(flat, jnp.int32),
            vmem(deformation_change.shape, f32),
            vmem(earlier_tension_state.shape, f32),
            vmem((1, cells), f32),
            vmem((27 * rows, LANES), f32),
            vmem((27 * rows, LANES), f32),
            vmem((STEPS, 2, 10 * size_y, LANES), f32),
            vmem((STEPS, 2, 10 * size_x, LANES), f32),
            vmem((STEPS, 2, rows, LANES), f32),
            vmem((STEPS, 2, 10 * size_y, LANES), f32),
            vmem((STEPS, 2, 10 * size_x, LANES), f32),
            vmem((STEPS, 2, rows, LANES), f32),
            vmem((GROUP * rows, LANES), f32),
            vmem((slots * 2 * GROUP + slots, rows * LANES), jnp.bfloat16),
            vmem((LANES, rows * LANES), jnp.bfloat16),
            vmem((peers,) + box, f32),
            vmem((max(peers - 1, 1),) + box, f32),
            vmem(earlier_tension_state.shape, f32),
            vmem((3, 8, cells), f32),
            pltpu.SemaphoreType.DMA((8,)),
            pltpu.SemaphoreType.DMA((3,)),
            pltpu.SemaphoreType.DMA((STEPS * 6,)),
            pltpu.SemaphoreType.DMA((STEPS * 6,)),
            pltpu.SemaphoreType.DMA((max(peers - 1, 1),)),
            pltpu.SemaphoreType.DMA((max(peers - 1, 1),)),
        ],
        compiler_params=pltpu.CompilerParams(collective_id=0, has_side_effects=True),
        name="slab",
    )(
        laid_tiers.reshape(1, 1),
        nodal_warmth_degrees.reshape(27 * rows, LANES),
        thermal_transfer_coefficient.reshape(flat),
        taken_beam_fraction.reshape(flat),
        holding_brick_column.reshape(flat),
        piece_onto_solid_brick.reshape(flat),
        deformation_change,
        earlier_tension_state,
        plastic_onset_threshold.reshape(1, cells),
    )
    return temp.reshape(nodal_warmth_degrees.shape), stress, forces


def solution(mesh):
    placed = (
        P(None, None, None, "gx", "gy", "gz"),
        P("gx", "gy", "gz"),
        P("gx", "gy", "gz"),
        P("gx", "gy", "gz"),
        P("gx", "gy", "gz", None, None),
        P("gx", "gy", "gz", None),
        P(None, None, ("gx", "gy", "gz")),
        P(None, None, ("gx", "gy", "gz")),
        P(("gx", "gy", "gz")),
    )
    counts_of = tuple(mesh.shape[name] for name in ("gx", "gy", "gz"))
    return jax.shard_map(
        functools.partial(local, counts_of),
        mesh=mesh,
        in_specs=placed,
        out_specs=(
            P(None, None, None, "gx", "gy", "gz"),
            P(None, None, ("gx", "gy", "gz")),
            P(None, None, ("gx", "gy", "gz")),
        ),
        check_vma=False,
    )
```

time: 245 us -> 27.1 us (0.11)
  the two profiles are of different devices: /device:TPU:10 before, /device:TPU:0 now
where the time goes in v1:
time: 27.1 us; the launch traced here: 26.9 us
  Pallas kernels  22.6 us (83%)
  local copies, waits for them, and re-layouts  3 us (11%)
  between operations  1.3 us (5%)
    pallas_call x1, Pallas kernels, local(): pl.pallas_call(functools.partial(kernel, block, counts_of, cells), out_sh...  22.6 us
    unnamed x7, local copies, waits for them, and re-layouts  3 us

profile of v1, /device:TPU:0, one launch (start us, length us, event | category | flops | bytes accessed | tf_op | source)
XLA Modules:
  0.0 26.9 jit_solution(8755707922490020471)
XLA Ops:
  1.3 22.6 %slab.1 = (f32[432,128]{1,0:T(8,128)}, f32[6,8,256]{2,1,0:T(8,128)}, f32[3,8,256]{2,1,0:T(8,128)}) custom-call(s32[1,1]{1,0:T(1,128)} %bitcast.8.tiers, f32[432,128]{1,0:T(8,128)} %bitcast.10, f32[16,128]{1,0:T(8,128)} %bitcast.11, f32[16,128]{1,0:T(8,128)} %bitcast.12, s32[16,128]{1,0:T(8,128)} %bitcast.13, s32[16,128]{1,0:T(8,128)} %bitcast.14, ...), custom_call_target="tpu_custom_call" | custom-call | tf_op jit(solution)/shard_map/slab/pallas_call | solution.py:561
  23.9 0.0 copy-start
  23.9 1.6 %copy.16 = f32[3,3,3,4,4,128]{5,4,3,2,1,0:T(4,128)} copy(f32[3,3,3,4,4,128]{5,4,3,2,1,0:T(4,128)} %bitcast.9) | data formatting | bytes 442368
  25.6 0.0 copy-done
  25.6 0.0 copy-start.1
  25.6 0.6 %copy.17 = f32[6,8,256]{2,1,0:T(8,128)} copy(f32[6,8,256]{2,1,0:T(8,128)S(1)} %copy-done) | data formatting | bytes 98304
  26.2 0.1 copy-done.1
  26.3 0.6 %copy.18 = f32[3,8,256]{2,1,0:T(8,128)} copy(f32[3,8,256]{2,1,0:T(8,128)S(1)} %copy-done.1) | data formatting | bytes 49152
Async XLA Ops:
  23.9 1.7 %copy-start = (f32[6,8,256]{2,1,0:T(8,128)S(1)}, f32[6,8,256]{2,1,0:T(8,128)}, u32[]{:S(2)}) copy-start(f32[6,8,256]{2,1,0:T(8,128)} %get-tuple-element.13) | copy-start | bytes 147460
  25.6 0.7 %copy-start.1 = (f32[3,8,256]{2,1,0:T(8,128)S(1)}, f32[3,8,256]{2,1,0:T(8,128)}, u32[]{:S(2)}) copy-start(f32[3,8,256]{2,1,0:T(8,128)} %get-tuple-element.14) | copy-start | bytes 73732

commit v2 on v1

--- a/solution.py
+++ b/solution.py
@@ -49,7 +49,7 @@
     block,
     counts_of,
     cells,
-    tiers,
+    tiers_hbm,
     warm_hbm,
     cond_hbm,
     beam_hbm,
@@ -58,9 +58,10 @@
     strain_hbm,
     stress_hbm,
     limit_hbm,
-    temp_out,
-    stress_out,
-    forces_out,
+    pong,
+    new_stress,
+    new_forces,
+    tiers,
     warm,
     cond,
     beam,
@@ -70,7 +71,6 @@
     stress,
     limit,
     ping,
-    pong,
     send_x,
     send_y,
     send_z,
@@ -82,10 +82,7 @@
     hot,
     outbox,
     inbox,
-    new_stress,
-    new_forces,
     in_sems,
-    out_sems,
     halo_send,
     halo_recv,
     trade_send,
@@ -105,6 +102,7 @@
         pltpu.make_async_copy(source, target, in_sems.at[index])
         for index, (source, target) in enumerate(
             (
+                (tiers_hbm, tiers),
                 (warm_hbm, warm),
                 (cond_hbm, cond),
                 (beam_hbm, beam),
@@ -120,11 +118,16 @@
         load.start()
 
     barrier = pltpu.get_barrier_semaphore()
-    for shift in range(1, peers):
-        pl.semaphore_signal(
-            barrier, inc=1, device_id={"gx": lax.rem(places[0] + shift, peers)}, device_id_type=MESH
-        )
-    for axis in (1, 2):
+    greet_all = peers - 1 > STEPS + 1
+    if greet_all:
+        for shift in range(1, peers):
+            pl.semaphore_signal(
+                barrier,
+                inc=1,
+                device_id={"gx": lax.rem(places[0] + shift, peers)},
+                device_id_type=MESH,
+            )
+    for axis in (1, 2) if greet_all else (0, 1, 2):
         for exists, move in ((has_lower[axis], -1), (has_upper[axis], 1)):
 
             @pl.when(exists)
@@ -160,9 +163,9 @@
     row_x = row // size_y
     row_y = row - row_x * size_y
 
-    for load in loads[:3]:
+    for load in loads[:4]:
         load.wait()
-    mask = (lane < tiers[0, 0]).astype(jnp.float32)
+    mask = (lane < tiers[0, 0, 0]).astype(jnp.float32)
     flow = cond[...] * mask
 
     send_x[0, 0, 9 * size_y : 10 * size_y] = flow[:size_y]
@@ -172,8 +175,8 @@
     send_y[0, 0, 9 * size_x : 10 * size_x] = hold[pl.ds(0, size_x, stride=size_y)]
     send_y[0, 1, 9 * size_x : 10 * size_x] = hold[pl.ds(size_y - 1, size_x, stride=size_y)]
 
-    neighbours = peers - 1
-    for axis in (1, 2):
+    neighbours = peers - 1 if greet_all else 0
+    for axis in (1, 2) if greet_all else (0, 1, 2):
         neighbours = neighbours + has_lower[axis].astype(jnp.int32) + has_upper[axis].astype(jnp.int32)
 
     def pack(current, step):
@@ -355,14 +358,14 @@
         return edges
 
     def label_rows():
-        for load in loads[3:5]:
+        for load in loads[4:6]:
             load.wait()
         low_iota = lax.broadcasted_iota(jnp.int32, (LANES, LANES), 0)
         slot_iota = lax.broadcasted_iota(jnp.int32, (slots, LANES), 0)
         cell = piece[...]
         chunk = cell // LANES
         low = cell - chunk * LANES
-        slot = jnp.where(lane < tiers[0, 0], owner[...] * chunks + chunk, -1)
+        slot = jnp.where(lane < tiers[0, 0, 0], owner[...] * chunks + chunk, -1)
         for r in range(rows):
             at = slice(r * LANES, (r + 1) * LANES)
             hot[:, at] = (low_iota == low[r : r + 1]).astype(jnp.float32).astype(jnp.bfloat16)
@@ -388,8 +391,6 @@
         fix(current, following, step, edges)
         current = following
 
-    write_temp = pltpu.make_async_copy(current, temp_out, out_sems.at[0])
-    write_temp.start()
 
     table = gauss_rows()
     for part in range(rows // GROUP):
@@ -455,7 +456,7 @@
         )
     for trade in trades:
         trade.start()
-    for load in loads[5:]:
+    for load in loads[6:]:
         load.wait()
     for trade in trades:
         trade.wait_recv()
@@ -514,10 +515,6 @@
             plane = shaped(sloped(fx, 0) , 1) + sloped(shaped(fy, 0), 1)
             new_forces[c, :, at] = shaped(plane, 2) + sloped(shaped(shaped(fz, 0), 1), 2)
 
-    write_stress = pltpu.make_async_copy(new_stress, stress_out, out_sems.at[1])
-    write_forces = pltpu.make_async_copy(new_forces, forces_out, out_sems.at[2])
-    write_stress.start()
-    write_forces.start()
     for trade in trades:
         trade.wait_send()
     for step in range(STEPS):
@@ -528,9 +525,18 @@
                 def _(step=step, axis=axis, up=up):
                     halo(step, axis, up).wait_send()
 
-    write_temp.wait()
-    write_stress.wait()
-    write_forces.wait()
+
+def write_out(temp, stress, forces, temp_out, stress_out, forces_out, sems):
+    copies = [
+        pltpu.make_async_copy(source, target, sems.at[index])
+        for index, (source, target) in enumerate(
+            ((temp, temp_out), (stress, stress_out), (forces, forces_out))
+        )
+    ]
+    for copy in copies:
+        copy.start()
+    for copy in copies:
+        copy.wait()
 
 
 def local(
@@ -558,16 +564,15 @@
     f32 = jnp.float32
     anywhere = pl.BlockSpec(memory_space=pl.ANY)
     vmem = pltpu.VMEM
-    temp, stress, forces = pl.pallas_call(
+    shapes = ((27 * rows, LANES), earlier_tension_state.shape, (3, 8, cells))
+    inside = pl.BlockSpec(memory_space=vmem)
+    results = pl.pallas_call(
         functools.partial(kernel, block, counts_of, cells),
-        out_shape=(
-            jax.ShapeDtypeStruct((27 * rows, LANES), f32),
-            jax.ShapeDtypeStruct(earlier_tension_state.shape, f32),
-            jax.ShapeDtypeStruct((3, 8, cells), f32),
-        ),
-        in_specs=[pl.BlockSpec(memory_space=pltpu.SMEM)] + [anywhere] * 8,
-        out_specs=(anywhere,) * 3,
+        out_shape=tuple(vmem(shape, f32) for shape in shapes),
+        in_specs=[pl.BlockSpec(memory_space=pltpu.HBM)] + [anywhere] * 8,
+        out_specs=(inside,) * 3,
         scratch_shapes=[
+            pltpu.SMEM((1, 1, 1), jnp.int32),
             vmem((27 * rows, LANES), f32),
             vmem(flat, f32),
             vmem(flat, f32),
@@ -576,7 +581,6 @@
             vmem(deformation_change.shape, f32),
             vmem(earlier_tension_state.shape, f32),
             vmem((1, cells), f32),
-            vmem((27 * rows, LANES), f32),
             vmem((27 * rows, LANES), f32),
             vmem((STEPS, 2, 10 * size_y, LANES), f32),
             vmem((STEPS, 2, 10 * size_x, LANES), f32),
@@ -589,10 +593,7 @@
             vmem((LANES, rows * LANES), jnp.bfloat16),
             vmem((peers,) + box, f32),
             vmem((max(peers - 1, 1),) + box, f32),
-            vmem(earlier_tension_state.shape, f32),
-            vmem((3, 8, cells), f32),
-            pltpu.SemaphoreType.DMA((8,)),
-            pltpu.SemaphoreType.DMA((3,)),
+            pltpu.SemaphoreType.DMA((9,)),
             pltpu.SemaphoreType.DMA((STEPS * 6,)),
             pltpu.SemaphoreType.DMA((STEPS * 6,)),
             pltpu.SemaphoreType.DMA((max(peers - 1, 1),)),
@@ -601,7 +602,7 @@
         compiler_params=pltpu.CompilerParams(collective_id=0, has_side_effects=True),
         name="slab",
     )(
-        laid_tiers.reshape(1, 1),
+        laid_tiers,
         nodal_warmth_degrees.reshape(27 * rows, LANES),
         thermal_transfer_coefficient.reshape(flat),
         taken_beam_fraction.reshape(flat),
@@ -611,6 +612,14 @@
         earlier_tension_state,
         plastic_onset_threshold.reshape(1, cells),
     )
+    temp, stress, forces = pl.pallas_call(
+        write_out,
+        out_shape=tuple(jax.ShapeDtypeStruct(shape, f32) for shape in shapes),
+        in_specs=[inside] * 3,
+        out_specs=(anywhere,) * 3,
+        scratch_shapes=[pltpu.SemaphoreType.DMA((3,))],
+        name="write_out",
+    )(*(pltpu.with_memory_space_constraint(result, vmem) for result in results))
     return temp.reshape(nodal_warmth_degrees.shape), stress, forces
 
 

time: 27.1 us -> 23.3 us (0.86)
  local copies, waits for them, and re-layouts: 3 us -> 0 us
  Pallas kernels: 22.6 us -> 21.9 us
    unnamed x7 -> x0, local copies, waits for them, and re-layouts: 3 us -> none
    pallas_call x1, Pallas kernels: 22.6 us -> 21.2 us  [local(): pl.pallas_call(functools.partial(kernel, block, counts_of, cells), out_sh...]
    pallas_call x0 -> x1, Pallas kernels: none -> 0.73 us  [local(): pl.pallas_call(write_out, out_shape=tuple((jax.ShapeDtypeStruct(shape, f3...]
where the time goes in v2:
time: 23.3 us; the launch traced here: 23.2 us
  Pallas kernels  21.9 us (94%)
  between operations  1.29 us (6%)
    pallas_call x1, Pallas kernels, local(): pl.pallas_call(functools.partial(kernel, block, counts_of, cells), out_sh...  21.2 us
    pallas_call x1, Pallas kernels, local(): pl.pallas_call(write_out, out_shape=tuple((jax.ShapeDtypeStruct(shape, f3...  0.73 us

profile of v2, /device:TPU:0, one launch (start us, length us, event | category | flops | bytes accessed | tf_op | source)
XLA Modules:
  0.0 23.2 jit_solution(1326567798235757403)
XLA Ops:
  1.3 21.2 %slab.1 = (f32[432,128]{1,0:T(8,128)S(1)}, f32[6,8,256]{2,1,0:T(8,128)S(1)}, f32[3,8,256]{2,1,0:T(8,128)S(1)}) custom-call(s32[1,1,1]{2,1,0:T(1,128)S(6)} %copy.12.tiers_hbm, f32[432,128]{1,0:T(8,128)} %bitcast.7, f32[16,128]{1,0:T(8,128)} %bitcast.8, f32[16,128]{1,0:T(8,128)} %bitcast.9, s32[16,128]{1,0:T(8,128)} %bitcast.10, s32[16,128]{1,0:T(8,128)} %bitcast.11, ...), custom_call_target="tpu_custom_call" | custom-call | tf_op jit(solution)/shard_map/slab/pallas_call | solution.py:569
  22.4 0.7 %write_out.1 = (f32[432,128]{1,0:T(8,128)}, f32[6,8,256]{2,1,0:T(8,128)}, f32[3,8,256]{2,1,0:T(8,128)}) custom-call(f32[432,128]{1,0:T(8,128)S(1)} %get-tuple-element.9.temp, f32[6,8,256]{2,1,0:T(8,128)S(1)} %get-tuple-element.10.stress, f32[3,8,256]{2,1,0:T(8,128)S(1)} %get-tuple-element.11.forces), custom_call_target="tpu_custom_call" | custom-call | tf_op jit(solution)/shard_map/write_out/pallas_call | solution.py:615

commit v3 on v2

--- a/solution.py
+++ b/solution.py
@@ -9,6 +9,7 @@
 from jax.sharding import PartitionSpec as P
 
 STEPS = 4
+PAIRS = STEPS // 2
 
 time_step = 0.003
 penalty = 3.0
@@ -77,16 +78,26 @@
     got_x,
     got_y,
     got_z,
+    corner_out,
+    corner_in,
     points,
     spread,
     hot,
+    tally,
     outbox,
     inbox,
+    count_out,
+    count_in,
     in_sems,
     halo_send,
     halo_recv,
     trade_send,
     trade_recv,
+    wide,
+    count_send,
+    count_recv,
+    corner_send,
+    corner_recv,
 ):
     size_x, size_y, size_z = block
     rows = size_x * size_y
@@ -98,12 +109,16 @@
     chunks = cells // LANES
     slots = peers * chunks
 
+    third = 9 * size_x * size_y
     loads = [
         pltpu.make_async_copy(source, target, in_sems.at[index])
         for index, (source, target) in enumerate(
             (
                 (tiers_hbm, tiers),
-                (warm_hbm, warm),
+                *(
+                    (warm_hbm.at[a * third : (a + 1) * third], warm.at[a * third : (a + 1) * third])
+                    for a in range(3)
+                ),
                 (cond_hbm, cond),
                 (beam_hbm, beam),
                 (owner_hbm, owner),
@@ -118,7 +133,7 @@
         load.start()
 
     barrier = pltpu.get_barrier_semaphore()
-    greet_all = peers - 1 > STEPS + 1
+    greet_all = peers - 1 > PAIRS + 1
     if greet_all:
         for shift in range(1, peers):
             pl.semaphore_signal(
@@ -135,6 +150,30 @@
                 pl.semaphore_signal(
                     barrier, inc=1, device_id={names[axis]: places[axis] + move}, device_id_type=MESH
                 )
+
+    exists_at = tuple(zip(has_lower, has_upper))
+    corners = []
+    for kind, (first, second) in enumerate(((0, 1), (0, 2), (1, 2))):
+        for s in range(2):
+            for t in range(2):
+                both = jnp.logical_and(exists_at[first][s], exists_at[second][t])
+                place = {
+                    names[first]: places[first] + 2 * s - 1,
+                    names[second]: places[second] + 2 * t - 1,
+                }
+                corners.append((4 * kind + 2 * s + t, 4 * kind + 3 - 2 * s - t, both, place))
+
+    for out_slot, _, both, place in corners:
+
+        @pl.when(both)
+        def _(place=place):
+            pl.semaphore_signal(barrier, inc=1, device_id=place, device_id_type=MESH)
+
+        @pl.when(jnp.logical_not(both))
+        def _(out_slot=out_slot):
+            corner_in[:, out_slot] = jnp.zeros(
+                corner_in.shape[:1] + corner_in.shape[2:], jnp.float32
+            )
 
     sends = (send_x, send_y, send_z)
     gots = (got_x, got_y, got_z)
@@ -163,7 +202,7 @@
     row_x = row // size_y
     row_y = row - row_x * size_y
 
-    for load in loads[:4]:
+    for load in loads[:6]:
         load.wait()
     mask = (lane < tiers[0, 0, 0]).astype(jnp.float32)
     flow = cond[...] * mask
@@ -178,6 +217,126 @@
     neighbours = peers - 1 if greet_all else 0
     for axis in (1, 2) if greet_all else (0, 1, 2):
         neighbours = neighbours + has_lower[axis].astype(jnp.int32) + has_upper[axis].astype(jnp.int32)
+
+    for _, _, both, _ in corners:
+        neighbours = neighbours + both.astype(jnp.int32)
+
+    def corner(pair, out_slot, in_slot, place):
+        return pltpu.make_async_remote_copy(
+            src_ref=corner_out.at[pair, out_slot],
+            dst_ref=corner_in.at[pair, in_slot],
+            send_sem=corner_send.at[pair * 12 + out_slot],
+            recv_sem=corner_recv.at[pair * 12 + in_slot],
+            device_id=place,
+            device_id_type=MESH,
+        )
+
+    def pack_corners(current, pair):
+        for s in range(2):
+            for t in range(2):
+                r = (0, rows - size_y)[s] + (0, size_y - 1)[t]
+                for c in range(3):
+                    at = (18 * s + 6 * t + c) * rows + r
+                    corner_out[pair, 2 * s + t, c : c + 1] = current[at : at + 1]
+                corner_out[pair, 2 * s + t, 3:4] = flow[r : r + 1]
+                edge = (0, LANES - 1)[t]
+                for kind in (1, 2):
+                    count = (size_y, size_x)[kind - 1]
+                    packed = None
+                    for n in range(4):
+                        if kind == 1:
+                            first = (0, rows - size_y)[s]
+                            if n == 3:
+                                value = flow[first : first + size_y]
+                            else:
+                                first = (18 * s + 3 * n + 2 * t) * rows + first
+                                value = current[first : first + size_y]
+                        else:
+                            first = (0, size_y - 1)[s]
+                            if n == 3:
+                                value = points[pl.ds(first, size_x, stride=size_y)]
+                            else:
+                                first = (9 * n + 6 * s + 2 * t) * rows + first
+                                value = current[pl.ds(first, size_x, stride=size_y)]
+                        shift = (n - edge) % LANES
+                        value = pltpu.roll(value, shift, 1) if shift else value
+                        packed = value if packed is None else jnp.where(lane[:count] == n, value, packed)
+                    corner_out[pair, 4 * kind + 2 * s + t, 0:count] = packed
+
+    def start_corners(pair):
+        for out_slot, in_slot, both, place in corners:
+
+            @pl.when(both)
+            def _(out_slot=out_slot, in_slot=in_slot, place=place):
+                corner(pair, out_slot, in_slot, place).start()
+
+    def arrive_corners(pair):
+        for out_slot, in_slot, both, place in corners:
+
+            @pl.when(both)
+            def _(out_slot=out_slot, in_slot=in_slot, place=place):
+                corner(pair, in_slot, out_slot, place).wait_recv()
+
+    def spread_lane(value, index):
+        return jnp.broadcast_to(value[:, index : index + 1], value.shape)
+
+    def foresee(pair):
+        now, then = 2 * pair, 2 * pair + 1
+        for s in range(2):
+            for got, sent, axis, count in ((got_x, send_x, 0, size_y), (got_y, send_y, 1, size_x)):
+                flow_beside = got[0, s, 9 * count : 10 * count]
+                for v in range(9):
+                    at = slice(v * count, (v + 1) * count)
+                    beside = got[now, s, at]
+                    value = got[then, s, at] + edges[axis][s] * (sent[now, s, at] - beside)
+                    t = (v % 3) // 2
+                    if v % 3 != 1:
+                        kind, n = 1 + axis, v // 3
+                        far = corner_in[pair, 4 * kind + 2 * s + t, 0:count]
+                        far_flow = corner_in[0, 4 * kind + 2 * s + t, 0:count]
+                        edge = (0, LANES - 1)[t]
+                        near_far = pair_coefficient(flow_beside, spread_lane(far_flow, 3))
+                        value = value + jnp.where(
+                            lane[:count] == edge, near_far * (spread_lane(far, n) - beside), 0.0
+                        )
+                    got[then, s, at] = value
+                for t in range(2):
+                    index = 2 * s + t if axis == 0 else 2 * t + s
+                    r = (0, count - 1)[t]
+                    weight = pair_coefficient(flow_beside[r : r + 1], corner_in[0, index, 3:4])
+                    for c in range(3):
+                        at = (6 * t + c) * count + r
+                        at = slice(at, at + 1)
+                        got[then, s, at] = got[then, s, at] + weight * (
+                            corner_in[pair, index, c : c + 1] - got[now, s, at]
+                        )
+            flow_beside = spread_lane(got_z[0, s], 9)
+            own = spread_lane(flow, (0, LANES - 1)[s])
+            beside = got_z[now, s]
+            got_z[then, s] = got_z[then, s] + pair_coefficient(own, flow_beside) * (
+                send_z[now, s] - beside
+            )
+            wide[...] = flow_beside
+            for t in range(2):
+                for kind, count in ((1, size_y), (2, size_x)):
+                    if kind == 1:
+                        first = (0, rows - size_y)[t]
+                        at = slice(first, first + size_y)
+                        lanes_of = [6 * t + n for n in range(3)]
+                    else:
+                        at = pl.ds((0, size_y - 1)[t], size_x, stride=size_y)
+                        lanes_of = [3 * n + 2 * t for n in range(3)]
+                    far = corner_in[pair, 4 * kind + 2 * t + s, 0:count]
+                    far_flow = spread_lane(corner_in[0, 4 * kind + 2 * t + s, 0:count], 3)
+                    weight = pair_coefficient(wide[at], far_flow)
+                    was = got_z.at[now, s][at]
+                    change = jnp.zeros((count, LANES), jnp.float32)
+                    for n in range(3):
+                        change = jnp.where(
+                            lane[:count] == lanes_of[n], weight * (spread_lane(far, n) - was), change
+                        )
+                    target = got_z.at[then, s]
+                    target[at] = target[at] + change
 
     def pack(current, step):
         for side, face in ((0, 0), (1, 2)):
@@ -211,17 +370,20 @@
                 def _(axis=axis, up=up):
                     halo(step, axis, up).start()
 
-    def arrive(step):
-        for axis in range(3):
-            for up, exists in ((False, has_upper[axis]), (True, has_lower[axis])):
-
-                @pl.when(exists)
-                def _(axis=axis, up=up):
-                    halo(step, axis, up).wait_recv()
-
+    def arrive(step, axis):
+        for up, exists in ((False, has_upper[axis]), (True, has_lower[axis])):
+
+            @pl.when(exists)
+            def _(up=up):
+                halo(step, axis, up).wait_recv()
+
+    edges = [None] * 3
+    points[0:rows] = flow
     pack(warm, 0)
     pl.semaphore_wait(barrier, neighbours)
     start(0)
+    pack_corners(warm, 0)
+    start_corners(0)
 
     def inner(value, axis):
         if axis == 0:
@@ -305,60 +467,50 @@
                 following[s0] += couples[axis][0] * (pltpu.roll(top, shift, along) - bottom)
                 following[s2] += couples[axis][1] * (pltpu.roll(bottom, span - shift, along) - top)
 
-    def fix(current, following, step, edges):
+    def fix(current, following, step, axis, edges):
         for side, face in ((0, 0), (1, 2)):
-            first = 0 if side == 0 else rows - size_y
-            for v, plane in enumerate(face_planes(0, face)):
-                at = slice(plane * rows + first, plane * rows + first + size_y)
-                beside = got_x[step, side, v * size_y : (v + 1) * size_y]
-                following[at] += edges[0][side] * (beside - current[at])
-            first = 0 if side == 0 else size_y - 1
-            for v, plane in enumerate(face_planes(1, face)):
-                at = pl.ds(plane * rows + first, size_x, stride=size_y)
-                beside = got_y[step, side, v * size_x : (v + 1) * size_x]
-                following[at] = following[at] + edges[1][side] * (beside - current[at])
-            first = 0 if side == 0 else LANES - 1
-            packed = got_z[step, side]
-            for v, plane in enumerate(face_planes(2, face)):
-                at = slice(plane * rows, (plane + 1) * rows)
-                shift = (first - v) % LANES
-                beside = pltpu.roll(packed, shift, 1) if shift else packed
-                following[at] += edges[2][side] * (beside - current[at])
-
-    def outer_couples():
-        points[0:rows] = flow
-        edges = []
-        edges.append(
-            [
+            packed = got_z[step, side] if axis == 2 else None
+            for v, plane in enumerate(face_planes(axis, face)):
+                if axis == 0:
+                    first = plane * rows + (0 if side == 0 else rows - size_y)
+                    at = slice(first, first + size_y)
+                    beside = got_x[step, side, v * size_y : (v + 1) * size_y]
+                elif axis == 1:
+                    at = pl.ds(plane * rows + (0 if side == 0 else size_y - 1), size_x, stride=size_y)
+                    beside = got_y[step, side, v * size_x : (v + 1) * size_x]
+                else:
+                    at = slice(plane * rows, (plane + 1) * rows)
+                    shift = ((0 if side == 0 else LANES - 1) - v) % LANES
+                    beside = pltpu.roll(packed, shift, 1) if shift else packed
+                following[at] = following[at] + edges[side] * (beside - current[at])
+
+    def outer_couples(axis):
+        if axis == 0:
+            return [
                 pair_coefficient(
                     flow[first : first + size_y], got_x[0, side, 9 * size_y : 10 * size_y]
                 )
                 for side, first in ((0, 0), (1, rows - size_y))
             ]
-        )
-        edges.append(
-            [
+        if axis == 1:
+            return [
                 pair_coefficient(
                     points[pl.ds(first, size_x, stride=size_y)],
                     got_y[0, side, 9 * size_x : 10 * size_x],
                 )
                 for side, first in ((0, 0), (1, size_y - 1))
             ]
-        )
-        edges.append(
-            [
-                jnp.where(
-                    lane == first,
-                    pair_coefficient(flow, pltpu.roll(got_z[0, side], (first - 9) % LANES, 1)),
-                    0.0,
-                )
-                for side, first in ((0, 0), (1, LANES - 1))
-            ]
-        )
-        return edges
+        return [
+            jnp.where(
+                lane == first,
+                pair_coefficient(flow, pltpu.roll(got_z[0, side], (first - 9) % LANES, 1)),
+                0.0,
+            )
+            for side, first in ((0, 0), (1, LANES - 1))
+        ]
 
     def label_rows():
-        for load in loads[4:6]:
+        for load in loads[6:8]:
             load.wait()
         low_iota = lax.broadcasted_iota(jnp.int32, (LANES, LANES), 0)
         slot_iota = lax.broadcasted_iota(jnp.int32, (slots, LANES), 0)
@@ -369,28 +521,65 @@
         for r in range(rows):
             at = slice(r * LANES, (r + 1) * LANES)
             hot[:, at] = (low_iota == low[r : r + 1]).astype(jnp.float32).astype(jnp.bfloat16)
-            spread[slots * 2 * GROUP :, at] = (
+            tally[:, at] = (
                 (slot_iota == slot[r : r + 1]).astype(jnp.float32).astype(jnp.bfloat16)
             )
+        counted = lax.dot_general(
+            tally[...], hot[...], (((1,), (1,)), ((), ())), preferred_element_type=jnp.float32
+        )
+        count_out[...] = jnp.zeros(count_out.shape, jnp.float32)
+        for o in range(peers):
+            count_out[o, 0:chunks] = counted[o * chunks : (o + 1) * chunks]
         return slot
 
+    def trade_of(source, target, send_sems, recv_sems):
+        copies = []
+        for shift in range(1, peers):
+            peer = lax.rem(places[0] + shift, peers)
+            copies.append(
+                pltpu.make_async_remote_copy(
+                    src_ref=source.at[peer],
+                    dst_ref=target.at[shift - 1],
+                    send_sem=send_sems.at[shift - 1],
+                    recv_sem=recv_sems.at[shift - 1],
+                    device_id={"gx": peer},
+                    device_id_type=MESH,
+                )
+            )
+        return copies
+
+    count_trades = trade_of(count_out, count_in, count_send, count_recv)
     slot = None
-    edges = None
     current = warm
-    for step in range(STEPS):
-        following = ping if step % 2 == 0 else pong
-        if step > 0:
-            pack(current, step)
-            start(step)
-        advance(current, following, step)
-        if step == 0:
+    for pair in range(PAIRS):
+        now, then = 2 * pair, 2 * pair + 1
+        middle = ping
+        if pair > 0:
+            pack(current, now)
+            start(now)
+            pack_corners(current, pair)
+            start_corners(pair)
+        advance(current, middle, now)
+        pack(middle, then)
+        start(then)
+        if pair == 0:
             slot = label_rows()
-        arrive(step)
-        if step == 0:
-            edges = outer_couples()
-        fix(current, following, step, edges)
-        current = following
-
+        for axis in (2, 0, 1):
+            arrive(now, axis)
+            if pair == 0:
+                edges[axis] = outer_couples(axis)
+            fix(current, middle, now, axis, edges[axis])
+        advance(middle, pong, then)
+        for axis in (2, 0, 1):
+            arrive(then, axis)
+        arrive_corners(pair)
+        if pair == PAIRS - 1:
+            for trade in count_trades:
+                trade.start()
+        foresee(pair)
+        for axis in (2, 0, 1):
+            fix(middle, pong, then, axis, edges[axis])
+        current = pong
 
     table = gauss_rows()
     for part in range(rows // GROUP):
@@ -437,28 +626,13 @@
                 total[s * 2 * GROUP : s * 2 * GROUP + GROUP]
                 + total[s * 2 * GROUP + GROUP : (s + 1) * 2 * GROUP]
             )
-        first = slots * 2 * GROUP + o * chunks
-        outbox[o, chunks * GROUP :] = jnp.zeros((outbox.shape[1] - chunks * GROUP, LANES), jnp.float32)
-        outbox[o, chunks * GROUP : chunks * GROUP + chunks] = total[first : first + chunks]
-
-    trades = []
-    for shift in range(1, peers):
-        peer = lax.rem(places[0] + shift, peers)
-        trades.append(
-            pltpu.make_async_remote_copy(
-                src_ref=outbox.at[peer],
-                dst_ref=inbox.at[shift - 1],
-                send_sem=trade_send.at[shift - 1],
-                recv_sem=trade_recv.at[shift - 1],
-                device_id={"gx": peer},
-                device_id_type=MESH,
-            )
-        )
+
+    trades = trade_of(outbox, inbox, trade_send, trade_recv)
     for trade in trades:
         trade.start()
-    for load in loads[6:]:
+    for load in loads[8:]:
         load.wait()
-    for trade in trades:
+    for trade in trades + count_trades:
         trade.wait_recv()
 
     point = lax.broadcasted_iota(jnp.int32, (GROUP, LANES), 0)
@@ -486,10 +660,10 @@
         at = slice(k * LANES, (k + 1) * LANES)
         own = pl.ds(k * GROUP, GROUP)
         sums = outbox[places[0], own]
-        count = outbox[places[0], pl.ds(chunks * GROUP + k, 1)]
+        count = count_out[places[0], pl.ds(k, 1)]
         for shift in range(1, peers):
             sums = sums + inbox[shift - 1, own]
-            count = count + inbox[shift - 1, pl.ds(chunks * GROUP + k, 1)]
+            count = count + count_in[shift - 1, pl.ds(k, 1)]
         thermal = sums / jnp.maximum(count, 1.0)
         normal = [strain[d, :, at] - expansion * thermal for d in range(3)]
         volume = normal[0] + normal[1] + normal[2]
@@ -515,8 +689,14 @@
             plane = shaped(sloped(fx, 0) , 1) + sloped(shaped(fy, 0), 1)
             new_forces[c, :, at] = shaped(plane, 2) + sloped(shaped(shaped(fz, 0), 1), 2)
 
-    for trade in trades:
+    for trade in trades + count_trades:
         trade.wait_send()
+    for pair in range(PAIRS):
+        for out_slot, in_slot, both, place in corners:
+
+            @pl.when(both)
+            def _(pair=pair, out_slot=out_slot, in_slot=in_slot, place=place):
+                corner(pair, out_slot, in_slot, place).wait_send()
     for step in range(STEPS):
         for axis in range(3):
             for up, exists in ((False, has_lower[axis]), (True, has_upper[axis])):
@@ -527,10 +707,16 @@
 
 
 def write_out(temp, stress, forces, temp_out, stress_out, forces_out, sems):
+    third = temp.shape[0] // 3
+    parts = [pl.ds(a * third, third) for a in range(3)]
     copies = [
         pltpu.make_async_copy(source, target, sems.at[index])
         for index, (source, target) in enumerate(
-            ((temp, temp_out), (stress, stress_out), (forces, forces_out))
+            (
+                *((temp.at[part], temp_out.at[part]) for part in parts),
+                (stress, stress_out),
+                (forces, forces_out),
+            )
         )
     ]
     for copy in copies:
@@ -559,7 +745,8 @@
     chunks = cells // LANES
     peers = counts_of[0]
     slots = peers * chunks
-    box = (chunks * GROUP + -(-chunks // GROUP) * GROUP, LANES)
+    box = (chunks * GROUP, LANES)
+    count_box = (-(-chunks // GROUP) * GROUP, LANES)
     flat = (rows, LANES)
     f32 = jnp.float32
     anywhere = pl.BlockSpec(memory_space=pl.ANY)
@@ -588,16 +775,26 @@
             vmem((STEPS, 2, 10 * size_y, LANES), f32),
             vmem((STEPS, 2, 10 * size_x, LANES), f32),
             vmem((STEPS, 2, rows, LANES), f32),
+            vmem((PAIRS, 12, max(4, size_x, size_y), LANES), f32),
+            vmem((PAIRS, 12, max(4, size_x, size_y), LANES), f32),
             vmem((GROUP * rows, LANES), f32),
-            vmem((slots * 2 * GROUP + slots, rows * LANES), jnp.bfloat16),
+            vmem((slots * 2 * GROUP, rows * LANES), jnp.bfloat16),
             vmem((LANES, rows * LANES), jnp.bfloat16),
+            vmem((slots, rows * LANES), jnp.bfloat16),
             vmem((peers,) + box, f32),
             vmem((max(peers - 1, 1),) + box, f32),
-            pltpu.SemaphoreType.DMA((9,)),
+            vmem((peers,) + count_box, f32),
+            vmem((max(peers - 1, 1),) + count_box, f32),
+            pltpu.SemaphoreType.DMA((11,)),
             pltpu.SemaphoreType.DMA((STEPS * 6,)),
             pltpu.SemaphoreType.DMA((STEPS * 6,)),
             pltpu.SemaphoreType.DMA((max(peers - 1, 1),)),
             pltpu.SemaphoreType.DMA((max(peers - 1, 1),)),
+            vmem(flat, f32),
+            pltpu.SemaphoreType.DMA((max(peers - 1, 1),)),
+            pltpu.SemaphoreType.DMA((max(peers - 1, 1),)),
+            pltpu.SemaphoreType.DMA((PAIRS * 12,)),
+            pltpu.SemaphoreType.DMA((PAIRS * 12,)),
         ],
         compiler_params=pltpu.CompilerParams(collective_id=0, has_side_effects=True),
         name="slab",
@@ -617,7 +814,7 @@
         out_shape=tuple(jax.ShapeDtypeStruct(shape, f32) for shape in shapes),
         in_specs=[inside] * 3,
         out_specs=(anywhere,) * 3,
-        scratch_shapes=[pltpu.SemaphoreType.DMA((3,))],
+        scratch_shapes=[pltpu.SemaphoreType.DMA((5,))],
         name="write_out",
     )(*(pltpu.with_memory_space_constraint(result, vmem) for result in results))
     return temp.reshape(nodal_warmth_degrees.shape), stress, forces

time: 23.3 us -> 20 us (0.86)
  Pallas kernels: 21.9 us -> 18.5 us
    pallas_call x1, Pallas kernels: 21.2 us -> 17.8 us  [local(): pl.pallas_call(functools.partial(kernel, block, counts_of, cells), out_sh...]
where the time goes in v3:
time: 20 us; the launch traced here: 19.8 us
  Pallas kernels  18.5 us (92%)
  between operations  1.29 us (6%)
    pallas_call x1, Pallas kernels, local(): pl.pallas_call(functools.partial(kernel, block, counts_of, cells), out_sh...  17.8 us
    pallas_call x1, Pallas kernels, local(): pl.pallas_call(write_out, out_shape=tuple((jax.ShapeDtypeStruct(shape, f3...  0.74 us

profile of v3, /device:TPU:0, one launch (start us, length us, event | category | flops | bytes accessed | tf_op | source)
XLA Modules:
  0.0 19.8 jit_solution(11194092082849524761)
XLA Ops:
  1.3 17.8 %slab.1 = (f32[432,128]{1,0:T(8,128)S(1)}, f32[6,8,256]{2,1,0:T(8,128)S(1)}, f32[3,8,256]{2,1,0:T(8,128)S(1)}) custom-call(s32[1,1,1]{2,1,0:T(1,128)S(6)} %copy.12.tiers_hbm, f32[432,128]{1,0:T(8,128)} %bitcast.7, f32[16,128]{1,0:T(8,128)} %bitcast.8, f32[16,128]{1,0:T(8,128)} %bitcast.9, s32[16,128]{1,0:T(8,128)} %bitcast.10, s32[16,128]{1,0:T(8,128)} %bitcast.11, ...), custom_call_target="tpu_custom_call" | custom-call | tf_op jit(solution)/shard_map/slab/pallas_call | solution.py:756
  19.1 0.7 %write_out.1 = (f32[432,128]{1,0:T(8,128)}, f32[6,8,256]{2,1,0:T(8,128)}, f32[3,8,256]{2,1,0:T(8,128)}) custom-call(f32[432,128]{1,0:T(8,128)S(1)} %get-tuple-element.9.temp, f32[6,8,256]{2,1,0:T(8,128)S(1)} %get-tuple-element.10.stress, f32[3,8,256]{2,1,0:T(8,128)S(1)} %get-tuple-element.11.forces), custom_call_target="tpu_custom_call" | custom-call | tf_op jit(solution)/shard_map/write_out/pallas_call | solution.py:812
